TPU v7x, 512 devices: a whole 4x8x8 slice. The times are simulated.
512 devices in a mesh: section: 16 (over z, core), tp: 32 (over x, y).
Axes of the slice: x: 4, y: 8, z: 8, core: 2. Of those that a mesh axis runs over, the one named last changes fastest.
Arguments:
- hidden: bfloat16 [16, 256, 8192], P('section', 'tp'), may hold values from -6 to 6
- norm_gain: float32 [16, 8192], P('section'), may hold values from 0.1 to 1.9
- w_query: bfloat16 [16, 8192, 4096], P('section', None, 'tp'), may hold values from -0.0625 to 0.0625
- w_keyval: bfloat16 [16, 1024, 8192], P('section', 'tp'), may hold values from -0.0625 to 0.0625
- w_out: bfloat16 [16, 4096, 8192], P('section', 'tp'), may hold values from -0.09375 to 0.09375
- kv_cache: bfloat16 [16, 128, 24, 1024], P('section', 'tp'), may hold values from -700 to 700
- owner_map: int32 [16, 64], P('section'), may hold values from 0 to 31, as said below
- accepted: int32 [16, 64], P('section'), may hold values from 0 to 4
- context: int32 [16, 64], P('section'), may hold values from 1 to 24
- draft_ids: int32 [16, 64, 4], P('section'), may hold values from 0 to 151935
Outputs:
- next_hidden: bfloat16 [16, 256, 8192], P('section', 'tp')
- committed_kv: bfloat16 [16, 512, 1024], P('section', 'tp')
- committed_ids: int32 [16, 512], P('section', 'tp')
Inputs may be any that keep to these rules, and one draw needn't show every extreme that they name: `owner_map`: in every window at most 4 requests share an owner, and some owner holds exactly 4.
All inputs are finite; a program needn't handle non-finite values.
Results may differ from a plain program's by a relative error of at most 0.017.
Values may be sent and summed in bfloat16 or wider, within the bound.
A program may use at most 64 MiB of HBM per device.

v0:
```python
import jax
import jax.numpy as jnp
from jax import lax
from jax.sharding import PartitionSpec as P

HEADS = 32
KVH = 4
HD = 128


epsilon = 1e-06


def passed_along(block, axis, distance):
    devices = range(lax.axis_size(axis))
    route = [((i - distance) % len(devices), i) for i in devices]
    return lax.ppermute(block, axis, route)


def owner_ranks(owners):
    count_all = owners.shape[0]
    same_owner = owners[:, None] == owners[None, :]
    position = jnp.arange(count_all, dtype=jnp.int32)
    earlier = position[None, :] < position[:, None]
    return jnp.sum(jnp.where(same_owner & earlier, 1, 0), axis=1).astype(jnp.int32)


def slot_requests(owners, capacity, groups):
    slot_of = owners * capacity + owner_ranks(owners)
    slot_total = groups * capacity
    matches = slot_of[None, :] == jnp.arange(slot_total, dtype=jnp.int32)[:, None]
    request_ids = jnp.arange(owners.shape[0], dtype=jnp.int32)
    found_ids = jnp.sum(jnp.where(matches, request_ids[None, :] + 1, 0), axis=1)
    return found_ids - 1


def attend(queries, new_pairs, cached, lengths):
    slot_count = queries.shape[0]
    draft_steps = queries.shape[1]
    cached_len = cached.shape[1]
    pair_width = cached.shape[2] // 2
    key_span = cached_len + draft_steps
    key_rows = jnp.concatenate([cached[:, :, :pair_width], new_pairs[:, :, :pair_width]], axis=1)
    values = jnp.concatenate([cached[:, :, pair_width:], new_pairs[:, :, pair_width:]], axis=1)
    key_rows = key_rows.reshape(slot_count, key_span, KVH, HD)
    values = values.reshape(slot_count, key_span, KVH, HD)
    grouped = queries.reshape(slot_count, draft_steps, KVH, HEADS // KVH, HD)
    scores = jnp.einsum(
        "sjkgd,spkd->skgjp", grouped, key_rows, preferred_element_type=jnp.float32
    ) * HD ** (-0.5)
    position = jnp.arange(key_span, dtype=jnp.int32)
    step_ids = jnp.arange(draft_steps, dtype=jnp.int32)
    cached_ok = (position[None, :] < lengths[:, None]) & (position[None, :] < cached_len)
    fresh_ok = (position[None, :] >= cached_len) & (
        position[None, :] - cached_len <= step_ids[:, None]
    )
    allowed = cached_ok[:, None, :] | fresh_ok[None, :, :]
    scores = jnp.where(allowed[:, None, None, :, :], scores, -jnp.inf)
    row_max = jnp.max(scores, axis=-1, keepdims=True)
    weights = jnp.exp(scores - row_max)
    probabilities = (weights / jnp.sum(weights, axis=-1, keepdims=True)).astype(jnp.bfloat16)
    attended = jnp.einsum(
        "skgjp,spkd->sjkgd", probabilities, values, preferred_element_type=jnp.float32
    )
    return attended.reshape(slot_count, draft_steps, HEADS * HD).astype(jnp.bfloat16)


def on_device(
    hidden, norm_gain, w_query, w_keyval, w_out, kv_cache, owner_map, accepted, context, draft_ids
):
    groups = lax.axis_size("tp")
    my_index = lax.axis_index("tp")
    owners = owner_map[0]
    accepts = accepted[0]
    lengths = context[0]
    token_ids = draft_ids[0]
    requests = owners.shape[0]
    draft_steps = token_ids.shape[1]
    per_device = requests // groups
    capacity = kv_cache.shape[1]
    query_cols = w_query.shape[2]
    pair_cols = w_keyval.shape[1]
    row_width = query_cols + pair_cols
    weight_query = w_query[0]
    weight_pair = w_keyval[0]
    weight_out = w_out[0]
    cached = kv_cache[0]
    rows_f32 = hidden[0].astype(jnp.float32)
    inverse_rms = lax.rsqrt(jnp.mean(rows_f32 * rows_f32, axis=1, keepdims=True) + epsilon)
    normed = (rows_f32 * inverse_rms * norm_gain[0][None, :]).astype(jnp.bfloat16)
    slot_of = owners * capacity + owner_ranks(owners)
    holders = slot_requests(owners, capacity, groups)
    safe_req = jnp.maximum(holders, 0)
    my_slots = lax.dynamic_slice_in_dim(holders, my_index * capacity, capacity)
    my_live = my_slots >= 0
    my_safe = jnp.maximum(my_slots, 0)
    step_ids = jnp.arange(draft_steps, dtype=jnp.int32)
    blocks = 1
    per_block = per_device // blocks
    kept_pairs = jnp.zeros((capacity, draft_steps, groups * pair_cols), jnp.bfloat16)
    row_piece = lax.all_gather(normed, "tp", axis=0, tiled=True)
    query_part = jnp.dot(row_piece, weight_query, preferred_element_type=jnp.float32).astype(
        jnp.bfloat16
    )
    pair_part = lax.dot_general(
        row_piece, weight_pair, (((1,), (1,)), ((), ())), preferred_element_type=jnp.float32
    ).astype(jnp.bfloat16)
    projected = jnp.concatenate([query_part, pair_part], axis=1)
    in_block = (holders >= 0) & (safe_req % per_device // per_block == 0)
    source_row = safe_req // per_device * per_block + (safe_req % per_device - 0)
    slot_flags = jnp.repeat(in_block, draft_steps)
    source = (source_row[:, None] * draft_steps + step_ids[None, :]).reshape(-1)
    source = jnp.where(slot_flags, source, 0)
    outgoing = jnp.take(projected, source, axis=0)
    outgoing = jnp.where(slot_flags[:, None], outgoing, jnp.zeros_like(outgoing))
    arrived = lax.all_to_all(outgoing, "tp", split_axis=0, concat_axis=1, tiled=True)
    arrived = arrived.reshape(capacity, draft_steps, groups, row_width)
    queries = arrived[:, :, :, :query_cols].reshape(capacity, draft_steps, groups * query_cols)
    new_pairs = arrived[:, :, :, query_cols:].reshape(capacity, draft_steps, groups * pair_cols)
    mine_block = my_live & (my_safe % per_device // per_block == 0)
    slot_lengths = jnp.where(mine_block, jnp.take(lengths, my_safe), 0)
    attended = attend(queries, new_pairs, cached, slot_lengths)
    flat_heads = attended.reshape(capacity * draft_steps, groups * query_cols)
    returned = lax.all_to_all(flat_heads, "tp", split_axis=1, concat_axis=0, tiled=True)
    block_requests = (
        jnp.arange(groups, dtype=jnp.int32)[:, None] * per_device
        + 0
        + jnp.arange(per_block, dtype=jnp.int32)[None, :]
    ).reshape(-1)
    target = (jnp.take(slot_of, block_requests)[:, None] * draft_steps + step_ids[None, :]).reshape(
        -1
    )
    heads_block = jnp.take(returned, target, axis=0)
    summed = lax.psum_scatter(
        jnp.dot(heads_block, weight_out, preferred_element_type=jnp.float32).astype(jnp.bfloat16),
        "tp",
        scatter_dimension=0,
        tiled=True,
    ).astype(jnp.float32)
    results = (rows_f32 + summed).astype(jnp.bfloat16)
    accept_now = mine_block[:, None] & (step_ids[None, :] < jnp.take(accepts, my_safe)[:, None])
    kept_pairs = jnp.where(accept_now[:, :, None], new_pairs, kept_pairs)
    shifted = passed_along(results, "section", 1)
    accept_all = my_live[:, None] & (step_ids[None, :] < jnp.take(accepts, my_safe)[:, None])
    kept_ids = jnp.where(accept_all, jnp.take(token_ids, my_safe, axis=0), -1).reshape(-1)
    committed = kept_pairs.reshape(capacity * draft_steps, groups * pair_cols)
    return (shifted[None], committed[None], kept_ids[None])


def solution(mesh):
    placed = (
        P("section", "tp", None),
        P("section", None),
        P("section", None, "tp"),
        P("section", "tp", None),
        P("section", "tp", None),
        P("section", "tp", None, None),
        P("section", None),
        P("section", None),
        P("section", None),
        P("section", None, None),
    )
    return jax.shard_map(
        on_device,
        mesh=mesh,
        in_specs=placed,
        out_specs=(P("section", "tp", None), P("section", "tp", None), P("section", "tp")),
        check_vma=False,
    )
```

profile of v0, /device:TPU:1, one launch (start us, length us, event | category | flops | bytes accessed | tf_op | source)
XLA Modules:
  0.0 388.9 jit_solution(7965786466616059564)
XLA Ops:
  7.2 1.2 fusion.13
  8.5 1.7 fusion.15
  10.2 0.1 add.270
  10.3 0.1 add.266
  10.5 0.9 select_reduce_fusion.1
  11.4 0.7 fusion.37
  12.0 0.1 select_reduce_fusion
  12.2 0.1 ne.83
  12.4 1.3 gather_fusion.5
  13.7 1.3 gather_fusion.4
  15.0 0.1 ge.60
  15.1 0.1 rem.77
  15.2 0.1 copy.46
  15.3 0.1 copy.47
  15.4 0.1 div.47
  15.7 0.7 multiply_add_fusion
  16.3 0.8 gather_fusion
  17.2 0.1 add.301
  17.3 0.1 add_select_fusion
  17.4 0.1 select_n.219
  18.0 82.7 %all-gather.2.cloned.1.call-done = bf16[256,8192]{1,0:T(8,128)(2,1)} async-done(((bf16[8,8192]{1,0:T(8,128)(2,1)}), bf16[256,8192]{1,0:T(8,128)(2,1)}) %all-gather.2.cloned.1.call-update) | async-done | bytes 4194320 | tf_op jit(solution)/shard_map/all_gather | solution.py:101
  100.7 3.8 convolution_convert_fusion.2
  104.6 3.2 fusion.9
  107.8 0.1 copy.51
  107.9 2.0 gather_fusion.1
  109.8 0.9 select_select_fusion
  110.7 6.1 %all-to-all-start = ((bf16[32,16,160]{2,1,0:T(8,128)(2,1)}), bf16[32,16,160]{2,1,0:T(8,128)(2,1)S(1)}, u32[]{:S(2)}, u32[]{:S(2)}) async-start(bf16[32,16,160]{2,1,0:T(8,128)(2,1)} %select_select_fusion), calls=%async_computation | async-start | bytes 524288 | tf_op jit(solution)/shard_map/all_to_all | solution.py:116
  116.9 9.7 %all-to-all-done = bf16[32,16,160]{2,1,0:T(8,128)(2,1)S(1)} async-done(((bf16[32,16,160]{2,1,0:T(8,128)(2,1)}), bf16[32,16,160]{2,1,0:T(8,128)(2,1)S(1)}, u32[]{:S(2)}, u32[]{:S(2)}) %all-to-all-start) | async-done | bytes 163872 | tf_op jit(solution)/shard_map/all_to_all | solution.py:116
  126.7 0.2 reshape.468
  127.0 0.2 fusion.6
  127.2 0.3 fusion.42
  127.5 0.9 fusion.8
  128.5 0.7 copy.59
  129.2 4.3 %all-to-all-start.1 = ((bf16[16,32,128]{2,0,1:T(8,128)(2,1)}), bf16[16,32,128]{2,0,1:T(8,128)(2,1)S(1)}, u32[]{:S(2)}, u32[]{:S(2)}) async-start(bf16[16,32,128]{2,0,1:T(8,128)(2,1)} %copy.59), calls=%async_computation.1 | async-start | bytes 262144 | tf_op jit(solution)/shard_map/all_to_all | solution.py:124
  133.6 0.1 add.276
  133.7 9.0 %all-to-all-done.1 = bf16[16,32,128]{2,0,1:T(8,128)(2,1)S(1)} async-done(((bf16[16,32,128]{2,0,1:T(8,128)(2,1)}), bf16[16,32,128]{2,0,1:T(8,128)(2,1)S(1)}, u32[]{:S(2)}, u32[]{:S(2)}) %all-to-all-start.1) | async-done | bytes 131104 | tf_op jit(solution)/shard_map/all_to_all | solution.py:124
  142.7 0.9 gather_fusion.2
  143.5 3.2 convolution_convert_fusion
  147.0 0.1 copy.60
  147.1 0.6 gather_fusion.3
  147.7 0.6 select_n.233
  148.3 0.2 reshape.471
  148.5 223.6 %reduce-scatter.2.cloned.1.call-done = bf16[8,8192]{1,0:T(8,128)(2,1)} async-done(((bf16[256,8192]{1,0:T(8,128)(2,1)}), bf16[8,8192]{1,0:T(8,128)(2,1)}) %reduce-scatter.2.cloned.1.call-update) | async-done | bytes 131088 | tf_op jit(solution)/shard_map/reduce_scatter | solution.py:134
  372.1 0.9 fusion.16
  373.1 6.4 %collective-permute-start = (bf16[8,8192]{1,0:T(8,128)(2,1)S(1)}, bf16[8,8192]{1,0:T(8,128)(2,1)S(1)}, u32[]{:S(2)}, u32[]{:S(2)}) collective-permute-start(bf16[8,8192]{1,0:T(8,128)(2,1)S(1)} %fusion.16), channel_id=1, source_target_pairs={{480,0},{0,32},{32,64},{64,96},{96,128},{128,160},{160,192},{192,2... | collective-permute-start | bytes 393224 | tf_op jit(solution)/shard_map/ppermute | solution.py:17
  379.4 0.7 broadcast_select_fusion
  380.1 1.3 collective-permute-done
  381.4 0.7 copy.78
  (59 shorter events, 1.6 us)
Async XLA Ops:
  7.2 136.4 %copy-start = (bf16[1,128,8192]{2,1,0:T(8,128)(2,1)S(1)}, bf16[1,128,8192]{2,1,0:T(8,128)(2,1)}, u32[]{:S(2)}) copy-start(bf16[1,128,8192]{2,1,0:T(8,128)(2,1)} %param.16) | copy-start | bytes 6291460
  7.2 93.5 %all-gather.2.cloned.1.call-start = ((), (), s32[]{:S(2)}) async-start(), calls=%async_computation.3 | async-start | bytes 4325376 | tf_op jit(solution)/shard_map/all_gather | solution.py:101
  100.7 3.8 copy-start.1
  104.5 12.3 %copy-start.3 = (bf16[1,4,24,1024]{3,2,1,0:T(8,128)(2,1)S(1)}, bf16[1,4,24,1024]{3,2,1,0:T(8,128)(2,1)}, u32[]{:S(2)}) copy-start(bf16[1,4,24,1024]{3,2,1,0:T(8,128)(2,1)} %param.17) | copy-start | bytes 589828
  110.7 15.9 %all-to-all-start = ((bf16[32,16,160]{2,1,0:T(8,128)(2,1)}), bf16[32,16,160]{2,1,0:T(8,128)(2,1)S(1)}, u32[]{:S(2)}, u32[]{:S(2)}) async-start(bf16[32,16,160]{2,1,0:T(8,128)(2,1)} %select_select_fusion), calls=%async_computation | async-start | bytes 524288 | tf_op jit(solution)/shard_map/all_to_all | solution.py:116
  129.2 13.5 %all-to-all-start.1 = ((bf16[16,32,128]{2,0,1:T(8,128)(2,1)}), bf16[16,32,128]{2,0,1:T(8,128)(2,1)S(1)}, u32[]{:S(2)}, u32[]{:S(2)}) async-start(bf16[16,32,128]{2,0,1:T(8,128)(2,1)} %copy.59), calls=%async_computation.1 | async-start | bytes 262144 | tf_op jit(solution)/shard_map/all_to_all | solution.py:124
  133.5 238.6 %reduce-scatter.2.cloned.1.call-start = ((), (), s32[]{:S(2)}) async-start(), calls=%async_computation.4 | async-start | bytes 4325376 | tf_op jit(solution)/shard_map/reduce_scatter | solution.py:134
  143.5 3.5 copy-start.4
  143.5 228.6 %copy-start.2 = (bf16[1,8,8192]{2,1,0:T(8,128)(2,1)S(1)}, bf16[1,8,8192]{2,1,0:T(8,128)(2,1)}, u32[]{:S(2)}) copy-start(bf16[1,8,8192]{2,1,0:T(8,128)(2,1)} %param.12) | copy-start | bytes 393220
  373.1 8.3 %collective-permute-start = (bf16[8,8192]{1,0:T(8,128)(2,1)S(1)}, bf16[8,8192]{1,0:T(8,128)(2,1)S(1)}, u32[]{:S(2)}, u32[]{:S(2)}) collective-permute-start(bf16[8,8192]{1,0:T(8,128)(2,1)S(1)} %fusion.16), channel_id=1, source_target_pairs={{480,0},{0,32},{32,64},{64,96},{96,128},{128,160},{160,192},{192,2... | collective-permute-start | bytes 393224 | tf_op jit(solution)/shard_map/ppermute | solution.py:17
Sparse Core Ops, SparseCore 0:
  11.7 88.9 all-gather.1
  146.9 225.1 reduce-scatter.1
where the time goes:
time: 390 us; the launch traced here: 389 us
  waiting for transfers between devices  326 us (84%)
  starting transfers between devices  16.9 us (4%)
  between operations  14.4 us (4%)
  matrix products  11.4 us (3%)
  local copies, waits for them, and re-layouts  11.1 us (3%)
  other arithmetic  8.87 us (2%)
    reduce_scatter x1, waiting for transfers between devices, on_device(): lax.psum_scatter(jnp.dot(heads_block, weight_out, preferred_element_type=...  224 us
    all_gather x1, waiting for transfers between devices, on_device(): row_piece = lax.all_gather(normed, 'tp', axis=0, tiled=True)  82.7 us
    all_to_all x1, waiting for transfers between devices, on_device(): lax.all_to_all(outgoing, 'tp', split_axis=0, concat_axis=1, tiled=True)  9.74 us
    all_to_all x1, waiting for transfers between devices, on_device(): lax.all_to_all(flat_heads, 'tp', split_axis=1, concat_axis=0, tiled=True)  8.97 us
  transfers between devices with their start and end apart: 5, of which 5 were waited for; matrix products, arithmetic and copies ran while one was open for 3% of the time, Pallas kernels for 0%

commit v1 on v0

--- a/solution.py
+++ b/solution.py
@@ -1,6 +1,8 @@
 import jax
 import jax.numpy as jnp
 from jax import lax
+from jax.experimental import pallas as pl
+from jax.experimental.pallas import tpu as pltpu
 from jax.sharding import PartitionSpec as P
 
 HEADS = 32
@@ -9,6 +11,248 @@
 
 
 epsilon = 1e-06
+
+
+NX = 4
+NY = 8
+LANES = 128
+XY_SHARE = 26 / 64
+
+
+def splits(width):
+    first = max(1, round(width // LANES * XY_SHARE)) * LANES
+    return ((0, first), (first, width - first))
+
+
+def far_positive(mode, axis, dx, dy):
+    if mode == 0:
+        return True if axis == 0 else dx % 2 == 0
+    return dy % 2 == 0 if axis == 0 else False
+
+
+def reach(mode, axis, sign, dx, dy):
+    half = (NX if axis == 0 else NY) // 2
+    return half if far_positive(mode, axis, dx, dy) == (sign > 0) else half - 1
+
+
+def travelled(mode, axis, dx, dy):
+    size = NX if axis == 0 else NY
+    ahead = (-dx if axis == 0 else -dy) % size
+    if ahead == 0:
+        return 0
+    if ahead <= reach(mode, axis, 1, dx, dy):
+        return ahead
+    return ahead - size
+
+
+def children(mode, dx, dy):
+    first, second = (0, 1) if mode == 0 else (1, 0)
+    hops = []
+    step1 = travelled(mode, first, dx, dy)
+    step2 = travelled(mode, second, dx, dy)
+    if step2 == 0:
+        for sign in (1, -1):
+            if step1 * sign >= 0 and abs(step1) < reach(mode, first, sign, dx, dy):
+                hops.append((first, sign))
+    for sign in (1, -1):
+        if step2 * sign >= 0 and abs(step2) < reach(mode, second, sign, dx, dy):
+            hops.append((second, sign))
+    return hops
+
+
+def moved(axis, sign, dx, dy):
+    return ((dx - sign) % NX, dy) if axis == 0 else (dx, (dy - sign) % NY)
+
+
+def parent(mode, dx, dy):
+    first, second = (0, 1) if mode == 0 else (1, 0)
+    step2 = travelled(mode, second, dx, dy)
+    axis = second if step2 else first
+    return (axis, 1 if travelled(mode, axis, dx, dy) > 0 else -1)
+
+
+def arrival_order(weights):
+    free = {}
+    order = []
+    pending = [(0.0, 0, 0, 0), (0.0, 1, 0, 0)]
+    while pending:
+        pending.sort()
+        now, mode, dx, dy = pending.pop(0)
+        order.append((mode, dx, dy))
+        for axis, sign in children(mode, dx, dy):
+            begin = max(now, free.get((axis, sign), 0.0))
+            free[axis, sign] = begin + weights[mode]
+            pending.append((begin + weights[mode] + 1.6, mode) + moved(axis, sign, dx, dy))
+    return order
+
+
+def place_of(dx, dy):
+    return dx * NY + dy
+
+
+def neighbours(mx, my):
+    return {
+        (0, 1): lax.rem(mx + 1, NX) * NY + my,
+        (0, -1): lax.rem(mx + NX - 1, NX) * NY + my,
+        (1, 1): mx * NY + lax.rem(my + 1, NY),
+        (1, -1): mx * NY + lax.rem(my + NY - 1, NY),
+    }
+
+
+def greet(devices):
+    barrier = pltpu.get_barrier_semaphore()
+    for device in devices:
+        pl.semaphore_signal(
+            barrier, inc=1, device_id={"tp": device}, device_id_type=pl.DeviceIdType.MESH
+        )
+    pl.semaphore_wait(barrier, len(devices))
+
+
+def block_at(mx, my, dx, dy):
+    return lax.rem(mx + dx, NX) * NY + lax.rem(my + dy, NY)
+
+
+def gather_kernel(x_ref, out_ref, send_sems, recv_sems):
+    me = lax.axis_index("tp")
+    mx = me // NY
+    my = lax.rem(me, NY)
+    near = neighbours(mx, my)
+    parts = splits(x_ref.shape[1])
+    greet(list(near.values()))
+
+    def copy(mode, dx, dy, link):
+        start, width = parts[mode]
+        there = moved(*link, dx, dy)
+        cols = pl.ds(start, width)
+        block = block_at(mx, my, dx, dy)
+        source = x_ref.at[:, cols] if (dx, dy) == (0, 0) else out_ref.at[block, :, cols]
+        return pltpu.make_async_remote_copy(
+            src_ref=source,
+            dst_ref=out_ref.at[block, :, cols],
+            send_sem=send_sems.at[mode, place_of(*there)],
+            recv_sem=recv_sems.at[mode, place_of(*there)],
+            device_id={"tp": near[link]},
+            device_id_type=pl.DeviceIdType.MESH,
+        )
+
+    started = []
+    order = arrival_order([part[1] * 16 / 46e3 for part in parts])
+    for mode, dx, dy in order:
+        if (dx, dy) != (0, 0):
+            link = parent(mode, dx, dy)
+            start, width = parts[mode]
+            cols = pl.ds(start, width)
+            block = block_at(mx, my, dx, dy)
+            pltpu.make_async_remote_copy(
+                src_ref=out_ref.at[block, :, cols],
+                dst_ref=out_ref.at[block, :, cols],
+                send_sem=send_sems.at[mode, place_of(dx, dy)],
+                recv_sem=recv_sems.at[mode, place_of(dx, dy)],
+                device_id={"tp": near[link]},
+                device_id_type=pl.DeviceIdType.MESH,
+            ).wait_recv()
+        for link in children(mode, dx, dy):
+            sent = copy(mode, dx, dy, link)
+            sent.start()
+            started.append(sent)
+    out_ref[me] = x_ref[...]
+    for sent in started:
+        sent.wait_send()
+
+
+def gather_rows(rows):
+    count, width = rows.shape
+    groups = NX * NY
+    out = pl.pallas_call(
+        gather_kernel,
+        out_shape=jax.ShapeDtypeStruct((groups, count, width), rows.dtype),
+        in_specs=[pl.BlockSpec(memory_space=pltpu.VMEM)],
+        out_specs=pl.BlockSpec(memory_space=pltpu.VMEM),
+        scratch_shapes=[
+            pltpu.SemaphoreType.DMA((2, groups)),
+            pltpu.SemaphoreType.DMA((2, groups)),
+        ],
+        compiler_params=pltpu.CompilerParams(collective_id=0, has_side_effects=True),
+    )(rows)
+    return out.reshape(groups * count, width)
+
+
+def reduce_kernel(p_ref, hid_ref, out_ref, got0, got1, stage0, stage1, send_sems, recv_sems):
+    me = lax.axis_index("tp")
+    mx = me // NY
+    my = lax.rem(me, NY)
+    near = neighbours(mx, my)
+    parts = splits(hid_ref.shape[1])
+    got = (got0, got1)
+    stage = (stage0, stage1)
+    greet(list(near.values()))
+    started = []
+
+    def total(mode, dx, dy):
+        start, width = parts[mode]
+        block = block_at(mx, my, dx, dy)
+        summed = p_ref[block, :, pl.ds(start, width)].astype(jnp.float32)
+        for link in children(mode, dx, dy):
+            slot = place_of(*moved(*link, dx, dy))
+            pltpu.make_async_remote_copy(
+                src_ref=stage[mode].at[slot],
+                dst_ref=got[mode].at[slot],
+                send_sem=send_sems.at[mode, slot],
+                recv_sem=recv_sems.at[mode, slot],
+                device_id={"tp": near[link]},
+                device_id_type=pl.DeviceIdType.MESH,
+            ).wait_recv()
+            summed = summed + got[mode][slot].astype(jnp.float32)
+        return summed
+
+    order = arrival_order([part[1] * 16 / 46e3 for part in parts])
+    for mode, dx, dy in reversed(order):
+        start, width = parts[mode]
+        if (dx, dy) == (0, 0):
+            cols = pl.ds(start, width)
+            summed = total(mode, dx, dy) + hid_ref[:, cols].astype(jnp.float32)
+            out_ref[:, cols] = summed.astype(out_ref.dtype)
+            continue
+        slot = place_of(dx, dy)
+        if children(mode, dx, dy):
+            stage[mode][slot] = total(mode, dx, dy).astype(jnp.bfloat16)
+            source = stage[mode].at[slot]
+        else:
+            source = p_ref.at[block_at(mx, my, dx, dy), :, pl.ds(start, width)]
+        axis, sign = parent(mode, dx, dy)
+        sent = pltpu.make_async_remote_copy(
+            src_ref=source,
+            dst_ref=got[mode].at[slot],
+            send_sem=send_sems.at[mode, slot],
+            recv_sem=recv_sems.at[mode, slot],
+            device_id={"tp": near[axis, -sign]},
+            device_id_type=pl.DeviceIdType.MESH,
+        )
+        sent.start()
+        started.append(sent)
+    for sent in started:
+        sent.wait_send()
+
+
+def reduce_rows(product, residual):
+    count, width = residual.shape
+    groups = NX * NY
+    parts = splits(width)
+    return pl.pallas_call(
+        reduce_kernel,
+        out_shape=jax.ShapeDtypeStruct((count, width), jnp.bfloat16),
+        in_specs=[pl.BlockSpec(memory_space=pltpu.VMEM)] * 2,
+        out_specs=pl.BlockSpec(memory_space=pltpu.VMEM),
+        scratch_shapes=[
+            pltpu.VMEM((groups, count, parts[0][1]), jnp.bfloat16),
+            pltpu.VMEM((groups, count, parts[1][1]), jnp.bfloat16),
+            pltpu.VMEM((groups, count, parts[0][1]), jnp.bfloat16),
+            pltpu.VMEM((groups, count, parts[1][1]), jnp.bfloat16),
+            pltpu.SemaphoreType.DMA((2, groups)),
+            pltpu.SemaphoreType.DMA((2, groups)),
+        ],
+        compiler_params=pltpu.CompilerParams(collective_id=1, has_side_effects=True),
+    )(product.reshape(groups, count, width), residual)
 
 
 def passed_along(block, axis, distance):
@@ -98,7 +342,7 @@
     blocks = 1
     per_block = per_device // blocks
     kept_pairs = jnp.zeros((capacity, draft_steps, groups * pair_cols), jnp.bfloat16)
-    row_piece = lax.all_gather(normed, "tp", axis=0, tiled=True)
+    row_piece = gather_rows(normed)
     query_part = jnp.dot(row_piece, weight_query, preferred_element_type=jnp.float32).astype(
         jnp.bfloat16
     )
@@ -131,13 +375,10 @@
         -1
     )
     heads_block = jnp.take(returned, target, axis=0)
-    summed = lax.psum_scatter(
-        jnp.dot(heads_block, weight_out, preferred_element_type=jnp.float32).astype(jnp.bfloat16),
-        "tp",
-        scatter_dimension=0,
-        tiled=True,
-    ).astype(jnp.float32)
-    results = (rows_f32 + summed).astype(jnp.bfloat16)
+    product = jnp.dot(heads_block, weight_out, preferred_element_type=jnp.float32).astype(
+        jnp.bfloat16
+    )
+    results = reduce_rows(product, hidden[0])
     accept_now = mine_block[:, None] & (step_ids[None, :] < jnp.take(accepts, my_safe)[:, None])
     kept_pairs = jnp.where(accept_now[:, :, None], new_pairs, kept_pairs)
     shifted = passed_along(results, "section", 1)

time: 390 us -> 138 us (0.35)
  waiting for transfers between devices: 326 us -> 15.6 us
  Pallas kernels: 0 us -> 68.5 us
  between operations: 14.4 us -> 1.05 us
  starting transfers between devices: 16.9 us -> 24.4 us
    reduce_scatter x1 -> x0, waiting for transfers between devices: 224 us -> none  [on_device(): lax.psum_scatter(jnp.dot(heads_block, weight_out, preferred_element_type=...]
    all_gather x1 -> x0, waiting for transfers between devices: 82.7 us -> none  [on_device(): row_piece = lax.all_gather(normed, 'tp', axis=0, tiled=True)]
    pallas_call x0 -> x2, Pallas kernels: none -> 68.5 us  [the longest x1 37.9 us: gather_rows(): pl.pallas_call(gather_kernel, out_shape=jax.ShapeDtypeStruct((groups, cou...]
    ppermute x1, starting transfers between devices: 6.36 us -> 15 us  [passed_along(): return lax.ppermute(block, axis, route)]
  transfers between devices with their start and end apart: 5 -> 3, of which waited for: 5 -> 3; matrix products, arithmetic and copies ran while one was open for 3% -> 4% of each run, Pallas kernels for 0% -> 0%
where the time goes in v1:
time: 138 us; the launch traced here: 137 us
  Pallas kernels  68.5 us (50%)
  starting transfers between devices  24.4 us (18%)
  waiting for transfers between devices  15.6 us (11%)
  matrix products  10.2 us (7%)
  local copies, waits for them, and re-layouts  9.77 us (7%)
  other arithmetic  7.25 us (5%)
    pallas_call x1, Pallas kernels, gather_rows(): pl.pallas_call(gather_kernel, out_shape=jax.ShapeDtypeStruct((groups, cou...  37.9 us
    pallas_call x1, Pallas kernels, reduce_rows(): pl.pallas_call(reduce_kernel, out_shape=jax.ShapeDtypeStruct((count, widt...  30.6 us
    ppermute x1, starting transfers between devices, passed_along(): return lax.ppermute(block, axis, route)  15 us
    all_to_all x1, waiting for transfers between devices, on_device(): lax.all_to_all(flat_heads, 'tp', split_axis=1, concat_axis=0, tiled=True)  8.17 us
    all_to_all x1, waiting for transfers between devices, on_device(): lax.all_to_all(outgoing, 'tp', split_axis=0, concat_axis=1, tiled=True)  5.89 us
    all_to_all x1, starting transfers between devices, on_device(): lax.all_to_all(outgoing, 'tp', split_axis=0, concat_axis=1, tiled=True)  4.93 us
    dot_general x1, matrix products, on_device(): jnp.dot(row_piece, weight_query, preferred_element_type=jnp.float32)  4.52 us
    all_to_all x1, starting transfers between devices, on_device(): lax.all_to_all(flat_heads, 'tp', split_axis=1, concat_axis=0, tiled=True)  4.47 us
  transfers between devices with their start and end apart: 3, of which 3 were waited for; matrix products, arithmetic and copies ran while one was open for 4% of the time, Pallas kernels for 0%

profile of v1, /device:TPU:1, one launch (start us, length us, event | category | flops | bytes accessed | tf_op | source)
XLA Modules:
  0.0 136.8 jit_solution(6280299005799533495)
XLA Ops:
  0.7 1.0 select_reduce_fusion.1
  1.7 0.7 fusion.45
  2.3 0.1 select_reduce_fusion
  2.5 0.1 rem.77
  2.6 0.1 div.47
  2.7 0.1 ne.83
  2.9 0.1 ge.60
  3.0 0.1 copy.46
  3.3 0.1 copy.47
  3.4 0.1 copy.50
  3.5 0.1 add_select_fusion
  3.6 0.1 select_n.219
  3.8 1.1 fusion.22
  4.9 1.7 %fusion.24.x_ref = bf16[8,8192]{1,0:T(8,128)(2,1)} fusion(f32[8192]{0:T(1024)} %bitcast.84, f32[8]{0:T(128)S(1)} %add_rsqrt_fusion, bf16[1,8,8192]{2,1,0:T(8,128)(2,1)} %param.12), kind=kLoop, calls=%fused_computation.29 | loop fusion | flops 262144 | bytes 294944 | tf_op jit(solution)/shard_map/convert_element_type | solution.py:334
  6.5 37.9 %shard_map.121 = bf16[32,8,8192]{2,1,0:T(8,128)(2,1)} custom-call(bf16[8,8192]{1,0:T(8,128)(2,1)} %fusion.24.x_ref), custom_call_target="tpu_custom_call" | custom-call | tf_op jit(solution)/shard_map/pallas_call | solution.py:166
  44.4 4.5 %fusion.13 = bf16[256,128]{0,1:T(8,128)(2,1)S(1)} fusion(bf16[1,8192,128]{2,1,0:T(8,128)(2,1)} %param.14, bf16[32,8,8192]{2,1,0:T(8,128)(2,1)} %shard_map.121), kind=kOutput, calls=%fused_computation.22 | convolution fusion | flops 536903680 | bytes 6356992 | tf_op jit(solution)/shard_map/dot_general | solution.py:346
  49.1 1.3 fusion.18
  50.4 0.1 copy.51
  50.5 2.0 %gather_fusion.1 = bf16[512,160]{1,0:T(8,128)(2,1)S(1)} fusion(bf16[256,160]{1,0:T(8,128)(2,1)S(1)} %copy.51, s32[1024]{0:T(1024)S(1)} %pad_clamp_fusion.2), kind=kCustom, calls=%fused_computation.3 | custom fusion | bytes 329728 | tf_op jit(solution)/shard_map/jit(_take)/gather | solution.py:358
  52.5 0.9 select_select_fusion
  53.4 4.9 %all-to-all-start = ((bf16[32,16,160]{2,1,0:T(8,128)(2,1)}), bf16[32,16,160]{2,1,0:T(8,128)(2,1)S(1)}, u32[]{:S(2)}, u32[]{:S(2)}) async-start(bf16[32,16,160]{2,1,0:T(8,128)(2,1)} %select_select_fusion), calls=%async_computation | async-start | bytes 524288 | tf_op jit(solution)/shard_map/all_to_all | solution.py:360
  58.5 0.1 add.265
  58.6 0.1 add.261
  58.8 0.6 gather_fusion.4
  59.4 0.6 gather_fusion.5
  60.1 0.8 gather_fusion
  61.0 0.1 add.296
  61.1 0.1 copy.60
  61.2 0.6 gather_fusion.3
  62.1 5.9 %all-to-all-done = bf16[32,16,160]{2,1,0:T(8,128)(2,1)S(1)} async-done(((bf16[32,16,160]{2,1,0:T(8,128)(2,1)}), bf16[32,16,160]{2,1,0:T(8,128)(2,1)S(1)}, u32[]{:S(2)}, u32[]{:S(2)}) %all-to-all-start) | async-done | bytes 163872 | tf_op jit(solution)/shard_map/all_to_all | solution.py:360
  68.1 0.2 reshape.473
  68.4 0.2 fusion.10
  68.6 0.3 fusion.50
  68.9 0.9 fusion.12
  69.8 0.7 copy.59
  70.6 4.5 %all-to-all-start.1 = ((bf16[16,32,128]{2,0,1:T(8,128)(2,1)}), bf16[16,32,128]{2,0,1:T(8,128)(2,1)S(1)}, u32[]{:S(2)}, u32[]{:S(2)}) async-start(bf16[16,32,128]{2,0,1:T(8,128)(2,1)} %copy.59), calls=%async_computation.1 | async-start | bytes 262144 | tf_op jit(solution)/shard_map/all_to_all | solution.py:368
  75.0 0.1 add.271
  75.1 0.1 and.178
  75.2 0.6 select_n.233
  75.8 0.2 reshape.477
  76.0 8.2 %all-to-all-done.1 = bf16[16,32,128]{2,0,1:T(8,128)(2,1)S(1)} async-done(((bf16[16,32,128]{2,0,1:T(8,128)(2,1)}), bf16[16,32,128]{2,0,1:T(8,128)(2,1)S(1)}, u32[]{:S(2)}, u32[]{:S(2)}) %all-to-all-start.1) | async-done | bytes 131104 | tf_op jit(solution)/shard_map/all_to_all | solution.py:368
  84.2 0.9 gather_fusion.2
  85.0 3.2 %fusion.1.p_ref = bf16[32,8,8192]{2,1,0:T(8,128)(2,1)} fusion(bf16[1,128,8192]{2,1,0:T(8,128)(2,1)S(1)} %copy-done, bf16[256,128]{1,0:T(8,128)(2,1)S(1)} %gather_fusion.2, pred[256]{0:T(512)(128)(4,1)S(1)} %compare_and_fusion.3), kind=kOutput, calls=%fused_computation.8 | convolution fusion | flops 539000832 | bytes 6357248 | tf_op jit(solution)/shard_map/dot_general | solution.py:378
  88.3 30.6 %shard_map.122 = bf16[8,8192]{1,0:T(8,128)(2,1)} custom-call(bf16[32,8,8192]{2,1,0:T(8,128)(2,1)} %fusion.1.p_ref, bf16[8,8192]{1,0:T(8,128)(2,1)} %bitcast.73), custom_call_target="tpu_custom_call" | custom-call | tf_op jit(solution)/shard_map/pallas_call | solution.py:241
  118.9 15.0 %collective-permute-start = (bf16[8,8192]{1,0:T(8,128)(2,1)}, bf16[8,8192]{1,0:T(8,128)(2,1)S(1)}, u32[]{:S(2)}, u32[]{:S(2)}) collective-permute-start(bf16[8,8192]{1,0:T(8,128)(2,1)} %shard_map.122), channel_id=1, source_target_pairs={{480,0},{0,32},{32,64},{64,96},{96,128},{128,160},{160,192},{192,2... | collective-permute-start | bytes 393224 | tf_op jit(solution)/shard_map/ppermute | solution.py:261
  133.9 0.7 broadcast_select_fusion
  134.6 1.6 %collective-permute-done = bf16[8,8192]{1,0:T(8,128)(2,1)S(1)} collective-permute-done((bf16[8,8192]{1,0:T(8,128)(2,1)}, bf16[8,8192]{1,0:T(8,128)(2,1)S(1)}, u32[]{:S(2)}, u32[]{:S(2)}) %collective-permute-start) | collective-permute-done | bytes 131104 | tf_op jit(solution)/shard_map/ppermute | solution.py:261
  136.2 0.7 copy.78
  (60 shorter events, 1.3 us)
Async XLA Ops:
  0.6 84.4 %copy-start = (bf16[1,128,8192]{2,1,0:T(8,128)(2,1)S(1)}, bf16[1,128,8192]{2,1,0:T(8,128)(2,1)}, u32[]{:S(2)}) copy-start(bf16[1,128,8192]{2,1,0:T(8,128)(2,1)} %param.16) | copy-start | bytes 6291460
  44.4 4.6 %copy-start.3 = (bf16[32,8,8192]{2,1,0:T(8,128)(2,1)S(1)}, bf16[32,8,8192]{2,1,0:T(8,128)(2,1)}, u32[]{:S(2)}) copy-start(bf16[32,8,8192]{2,1,0:T(8,128)(2,1)} %shard_map.121) | copy-start | bytes 12582916
  44.4 4.6 %copy-start.4 = (bf16[1,32,8192]{2,1,0:T(8,128)(2,1)S(1)}, bf16[1,32,8192]{2,1,0:T(8,128)(2,1)}, u32[]{:S(2)}) copy-start(bf16[1,32,8192]{2,1,0:T(8,128)(2,1)} %param.15) | copy-start | bytes 1572868
  49.0 9.4 %copy-start.7 = (s32[1,64]{1,0:T(1,128)S(1)}, s32[1,64]{1,0:T(1,128)}, u32[]{:S(2)}) copy-start(s32[1,64]{1,0:T(1,128)} %param.18) | copy-start | bytes 772
  49.0 9.8 %copy-start.1 = (s32[1,64]{1,0:T(1,128)S(1)}, s32[1,64]{1,0:T(1,128)}, u32[]{:S(2)}) copy-start(s32[1,64]{1,0:T(1,128)} %param.20) | copy-start | bytes 772
  49.0 10.4 %copy-start.2 = (s32[1,64]{1,0:T(1,128)S(1)}, s32[1,64]{1,0:T(1,128)}, u32[]{:S(2)}) copy-start(s32[1,64]{1,0:T(1,128)} %param.19) | copy-start | bytes 772
  49.0 12.1 %copy-start.6 = (s32[1,64,4]{1,2,0:T(4,128)S(1)}, s32[1,64,4]{1,2,0:T(4,128)}, u32[]{:S(2)}) copy-start(s32[1,64,4]{1,2,0:T(4,128)} %param.21) | copy-start | bytes 3076
  49.0 13.0 %copy-start.5 = (bf16[1,4,24,1024]{3,2,1,0:T(8,128)(2,1)S(1)}, bf16[1,4,24,1024]{3,2,1,0:T(8,128)(2,1)}, u32[]{:S(2)}) copy-start(bf16[1,4,24,1024]{3,2,1,0:T(8,128)(2,1)} %param.17) | copy-start | bytes 589828
  53.4 14.6 %all-to-all-start = ((bf16[32,16,160]{2,1,0:T(8,128)(2,1)}), bf16[32,16,160]{2,1,0:T(8,128)(2,1)S(1)}, u32[]{:S(2)}, u32[]{:S(2)}) async-start(bf16[32,16,160]{2,1,0:T(8,128)(2,1)} %select_select_fusion), calls=%async_computation | async-start | bytes 524288 | tf_op jit(solution)/shard_map/all_to_all | solution.py:360
  70.6 13.6 %all-to-all-start.1 = ((bf16[16,32,128]{2,0,1:T(8,128)(2,1)}), bf16[16,32,128]{2,0,1:T(8,128)(2,1)S(1)}, u32[]{:S(2)}, u32[]{:S(2)}) async-start(bf16[16,32,128]{2,0,1:T(8,128)(2,1)} %copy.59), calls=%async_computation.1 | async-start | bytes 262144 | tf_op jit(solution)/shard_map/all_to_all | solution.py:368
  118.9 17.3 %collective-permute-start = (bf16[8,8192]{1,0:T(8,128)(2,1)}, bf16[8,8192]{1,0:T(8,128)(2,1)S(1)}, u32[]{:S(2)}, u32[]{:S(2)}) collective-permute-start(bf16[8,8192]{1,0:T(8,128)(2,1)} %shard_map.122), channel_id=1, source_target_pairs={{480,0},{0,32},{32,64},{64,96},{96,128},{128,160},{160,192},{192,2... | collective-permute-start | bytes 393224 | tf_op jit(solution)/shard_map/ppermute | solution.py:261

commit v2 on v1

v2 whole, which is shorter than its diff:
```python
import jax
import jax.numpy as jnp
from jax import lax
from jax.experimental import pallas as pl
from jax.experimental.pallas import tpu as pltpu
from jax.sharding import PartitionSpec as P

HEADS = 32
KVH = 4
HD = 128


epsilon = 1e-06


NX = 4
NY = 8
LANES = 128
XY_SHARE = 26 / 64


def splits(width):
    first = max(1, round(width // LANES * XY_SHARE)) * LANES
    return ((0, first), (first, width - first))


def far_positive(mode, axis, dx, dy):
    if mode == 0:
        return True if axis == 0 else dx % 2 == 0
    return dy % 2 == 0 if axis == 0 else False


def reach(mode, axis, sign, dx, dy):
    half = (NX if axis == 0 else NY) // 2
    return half if far_positive(mode, axis, dx, dy) == (sign > 0) else half - 1


def travelled(mode, axis, dx, dy):
    size = NX if axis == 0 else NY
    ahead = (-dx if axis == 0 else -dy) % size
    if ahead == 0:
        return 0
    if ahead <= reach(mode, axis, 1, dx, dy):
        return ahead
    return ahead - size


def children(mode, dx, dy):
    first, second = (0, 1) if mode == 0 else (1, 0)
    hops = []
    step1 = travelled(mode, first, dx, dy)
    step2 = travelled(mode, second, dx, dy)
    if step2 == 0:
        for sign in (1, -1):
            if step1 * sign >= 0 and abs(step1) < reach(mode, first, sign, dx, dy):
                hops.append((first, sign))
    for sign in (1, -1):
        if step2 * sign >= 0 and abs(step2) < reach(mode, second, sign, dx, dy):
            hops.append((second, sign))
    return hops


def moved(axis, sign, dx, dy):
    return ((dx - sign) % NX, dy) if axis == 0 else (dx, (dy - sign) % NY)


def parent(mode, dx, dy):
    first, second = (0, 1) if mode == 0 else (1, 0)
    step2 = travelled(mode, second, dx, dy)
    axis = second if step2 else first
    return (axis, 1 if travelled(mode, axis, dx, dy) > 0 else -1)


def arrival_order(weights):
    free = {}
    order = []
    pending = [(0.0, 0, 0, 0), (0.0, 1, 0, 0)]
    while pending:
        pending.sort()
        now, mode, dx, dy = pending.pop(0)
        order.append((mode, dx, dy))
        for axis, sign in children(mode, dx, dy):
            begin = max(now, free.get((axis, sign), 0.0))
            free[axis, sign] = begin + weights[mode]
            pending.append((begin + weights[mode] + 1.6, mode) + moved(axis, sign, dx, dy))
    return order


def place_of(dx, dy):
    return dx * NY + dy


def neighbours(mx, my):
    return {
        (0, 1): lax.rem(mx + 1, NX) * NY + my,
        (0, -1): lax.rem(mx + NX - 1, NX) * NY + my,
        (1, 1): mx * NY + lax.rem(my + 1, NY),
        (1, -1): mx * NY + lax.rem(my + NY - 1, NY),
    }


def greet(devices):
    barrier = pltpu.get_barrier_semaphore()
    for device in devices:
        pl.semaphore_signal(
            barrier, inc=1, device_id={"tp": device}, device_id_type=pl.DeviceIdType.MESH
        )
    pl.semaphore_wait(barrier, len(devices))


def block_at(mx, my, dx, dy):
    return lax.rem(mx + dx, NX) * NY + lax.rem(my + dy, NY)


def slot_matrix(slot_ref, rows):
    row = lax.broadcasted_iota(jnp.int32, (rows, slot_ref.shape[1]), 0)
    return jnp.where(row == slot_ref[...], 1.0, 0.0).astype(jnp.bfloat16)


def project_kernel(
    hid_ref, gain_ref, slot_ref, wq_hbm, wp_hbm, out_ref,
    x_ref, all_ref, wq_ref, wp_ref, acc_ref, load_sems, send_sems, recv_sems,
):
    me = lax.axis_index("tp")
    mx = me // NY
    my = lax.rem(me, NY)
    near = neighbours(mx, my)
    width = hid_ref.shape[1]
    parts = splits(width)
    loads = [
        pltpu.make_async_copy(wq_hbm, wq_ref, load_sems.at[0]),
        pltpu.make_async_copy(wp_hbm, wp_ref, load_sems.at[1]),
    ]
    for load in loads:
        load.start()
    rows = hid_ref[...].astype(jnp.float32)
    inverse_rms = lax.rsqrt(jnp.mean(rows * rows, axis=1, keepdims=True) + epsilon)
    x_ref[...] = (rows * inverse_rms * gain_ref[...]).astype(jnp.bfloat16)
    greet(list(near.values()))

    def copy(mode, dx, dy, link):
        start, size = parts[mode]
        there = place_of(*moved(*link, dx, dy))
        cols = pl.ds(start, size)
        block = block_at(mx, my, dx, dy)
        source = x_ref.at[:, cols] if (dx, dy) == (0, 0) else all_ref.at[block, :, cols]
        return pltpu.make_async_remote_copy(
            src_ref=source,
            dst_ref=all_ref.at[block, :, cols],
            send_sem=send_sems.at[mode, there],
            recv_sem=recv_sems.at[mode, there],
            device_id={"tp": near[link]},
            device_id_type=pl.DeviceIdType.MESH,
        )

    started = []
    order = arrival_order([part[1] * 16 / 46e3 for part in parts])
    for mode, dx, dy in order:
        if (dx, dy) != (0, 0):
            start, size = parts[mode]
            landed = all_ref.at[block_at(mx, my, dx, dy), :, pl.ds(start, size)]
            pltpu.make_async_remote_copy(
                src_ref=landed,
                dst_ref=landed,
                send_sem=send_sems.at[mode, place_of(dx, dy)],
                recv_sem=recv_sems.at[mode, place_of(dx, dy)],
                device_id={"tp": near[parent(mode, dx, dy)]},
                device_id_type=pl.DeviceIdType.MESH,
            ).wait_recv()
        for link in children(mode, dx, dy):
            sent = copy(mode, dx, dy, link)
            sent.start()
            started.append(sent)
        if len(started) == 8:
            all_ref[me] = x_ref[...]
            for load in loads:
                load.wait()
    groups, count = all_ref.shape[:2]
    tokens = groups * count
    query_cols = wq_ref.shape[1]
    pair_cols = wp_ref.shape[0]
    step = width // 8
    acc_ref[...] = jnp.zeros_like(acc_ref)

    def add(k, carry):
        cols = pl.ds(pl.multiple_of(k * step, step), step)
        x = all_ref[:, :, cols].reshape(tokens, step)
        acc_ref[:, :query_cols] += jnp.dot(
            x, wq_ref[cols, :], preferred_element_type=jnp.float32
        )
        acc_ref[:, query_cols:] += lax.dot_general(
            x, wp_ref[:, cols], (((1,), (1,)), ((), ())), preferred_element_type=jnp.float32
        )
        return carry

    lax.fori_loop(0, 8, add, 0)
    queries = acc_ref[:, :query_cols].astype(jnp.bfloat16)
    pairs = acc_ref[:, query_cols:].astype(jnp.bfloat16)
    lane = lax.broadcasted_iota(jnp.int32, (pair_cols, LANES), 1)
    source = lax.broadcasted_iota(jnp.int32, (pair_cols, LANES), 0)
    offset = lax.rem(me, LANES // pair_cols) * pair_cols
    spread = jnp.where(lane == source + offset, 1.0, 0.0).astype(jnp.bfloat16)
    placed = jnp.dot(pairs, spread, preferred_element_type=jnp.float32).astype(jnp.bfloat16)
    chosen = slot_matrix(slot_ref, out_ref.shape[0] * out_ref.shape[1])
    out_shape = out_ref.shape[:2] + (LANES,)
    out_ref[:, :, :LANES] = (
        jnp.dot(chosen, queries, preferred_element_type=jnp.float32)
        .reshape(out_shape).astype(jnp.bfloat16)
    )
    out_ref[:, :, LANES:] = (
        jnp.dot(chosen, placed, preferred_element_type=jnp.float32)
        .reshape(out_shape).astype(jnp.bfloat16)
    )
    for sent in started:
        sent.wait_send()


def project_rows(hidden, gain, slot_tokens, weight_query, weight_pair, slot_rows):
    count, width = hidden.shape
    groups = NX * NY
    vmem = pl.BlockSpec(memory_space=pltpu.VMEM)
    hbm = pl.BlockSpec(memory_space=pl.ANY)
    query_cols = weight_query.shape[1]
    pair_cols = weight_pair.shape[0]
    return pl.pallas_call(
        project_kernel,
        out_shape=jax.ShapeDtypeStruct((groups, slot_rows, 2 * LANES), jnp.bfloat16),
        in_specs=[vmem, vmem, vmem, hbm, hbm],
        out_specs=vmem,
        scratch_shapes=[
            pltpu.VMEM((count, width), jnp.bfloat16),
            pltpu.VMEM((groups, count, width), jnp.bfloat16),
            pltpu.VMEM(weight_query.shape, jnp.bfloat16),
            pltpu.VMEM(weight_pair.shape, jnp.bfloat16),
            pltpu.VMEM((groups * count, query_cols + pair_cols), jnp.float32),
            pltpu.SemaphoreType.DMA((2,)),
            pltpu.SemaphoreType.DMA((2, groups)),
            pltpu.SemaphoreType.DMA((2, groups)),
        ],
        compiler_params=pltpu.CompilerParams(collective_id=0, has_side_effects=True),
    )(hidden, gain, slot_tokens, weight_query, weight_pair)


def attend_kernel(len_ref, got_ref, cache_ref, out_ref, pairs_ref):
    slot_rows = got_ref.shape[1]
    slots = len_ref.shape[0]
    steps = slot_rows // slots
    cached_rows = cache_ref.shape[0]
    cached_len = cached_rows // slots
    span = cached_rows + slot_rows
    per_kv = HEADS // KVH
    rows = per_kv * slot_rows
    row = lax.rem(lax.broadcasted_iota(jnp.int32, (rows, span), 0), slot_rows)
    col = lax.broadcasted_iota(jnp.int32, (rows, span), 1)
    fresh = col - cached_rows
    allowed = (fresh >= 0) & (fresh // steps == row // steps) & (fresh <= row)
    for slot in range(slots):
        base = slot * cached_len
        allowed |= (row // steps == slot) & (col >= base) & (col < base + len_ref[slot])
    pieces = got_ref.shape[0] // (2 * KVH)
    for e in range(KVH):
        cols = slice(e * HD, (e + 1) * HD)
        value_cols = slice((KVH + e) * HD, (KVH + e + 1) * HD)

        def joined(first):
            total = got_ref[first, :, LANES:].astype(jnp.float32)
            for i in range(1, pieces):
                total = total + got_ref[first + i, :, LANES:].astype(jnp.float32)
            return total.astype(jnp.bfloat16)

        new_keys = joined(e * pieces)
        new_values = joined((KVH + e) * pieces)
        pairs_ref[:, cols] = new_keys
        pairs_ref[:, value_cols] = new_values
        keys = jnp.concatenate([cache_ref[:, cols], new_keys], axis=0)
        values = jnp.concatenate([cache_ref[:, value_cols], new_values], axis=0)
        queries = got_ref[e * per_kv : (e + 1) * per_kv, :, :LANES].reshape(rows, HD)
        scores = lax.dot_general(
            queries, keys, (((1,), (1,)), ((), ())), preferred_element_type=jnp.float32
        ) * HD ** (-0.5)
        scores = jnp.where(allowed, scores, -jnp.inf)
        weights = jnp.exp(scores - jnp.max(scores, axis=1, keepdims=True))
        probs = (weights / jnp.sum(weights, axis=1, keepdims=True)).astype(jnp.bfloat16)
        attended = jnp.dot(probs, values, preferred_element_type=jnp.float32)
        out_ref[e * per_kv : (e + 1) * per_kv] = attended.reshape(
            per_kv, slot_rows, HD
        ).astype(jnp.bfloat16)


def attend_slots(lengths, arrived, cached):
    groups, slot_rows, _ = arrived.shape
    slots, cached_len, width = cached.shape
    vmem = pl.BlockSpec(memory_space=pltpu.VMEM)
    return pl.pallas_call(
        attend_kernel,
        out_shape=(
            jax.ShapeDtypeStruct((groups, slot_rows, HD), jnp.bfloat16),
            jax.ShapeDtypeStruct((slot_rows, width), jnp.bfloat16),
        ),
        in_specs=[pl.BlockSpec(memory_space=pltpu.SMEM), vmem, vmem],
        out_specs=(vmem, vmem),
    )(lengths, arrived, cached.reshape(slots * cached_len, width))


def reduce_kernel(
    slot_ref, heads_ref, hid_ref, wo_hbm, out_ref,
    p_ref, wo_ref, res_ref, got0, got1, stage0, stage1,
    load_sem, shift_send, shift_recv, send_sems, recv_sems,
):
    me = lax.axis_index("tp")
    section = lax.axis_index("section")
    sections = lax.axis_size("section")
    after = lax.rem(section + 1, sections)
    before = lax.rem(section + sections - 1, sections)
    mx = me // NY
    my = lax.rem(me, NY)
    near = neighbours(mx, my)
    width = hid_ref.shape[1]
    parts = splits(width)
    got = (got0, got1)
    stage = (stage0, stage1)
    load = pltpu.make_async_copy(wo_hbm, wo_ref, load_sem)
    load.start()
    barrier = pltpu.get_barrier_semaphore()
    for device in near.values():
        pl.semaphore_signal(
            barrier, inc=1, device_id={"tp": device}, device_id_type=pl.DeviceIdType.MESH
        )
    pl.semaphore_signal(
        barrier, inc=1, device_id={"section": before}, device_id_type=pl.DeviceIdType.MESH
    )
    groups, count = p_ref.shape[:2]
    tokens = groups * count
    slot_rows = heads_ref.shape[0] * heads_ref.shape[1]
    chosen = slot_matrix(slot_ref, slot_rows)
    heads = lax.dot_general(
        chosen, heads_ref[...].reshape(slot_rows, heads_ref.shape[2]),
        (((0,), (0,)), ((), ())), preferred_element_type=jnp.float32,
    ).astype(jnp.bfloat16)
    load.wait()
    step = 256

    def multiply(mode):
        start, size = parts[mode]

        def one(k, carry):
            cols = pl.ds(pl.multiple_of(start + k * step, LANES), step)
            piece = jnp.dot(heads, wo_ref[:, cols], preferred_element_type=jnp.float32)
            p_ref[:, :, cols] = piece.reshape(groups, count, step).astype(jnp.bfloat16)
            return carry

        lax.fori_loop(0, size // step, one, 0)

    started = []

    def total(mode, dx, dy):
        start, size = parts[mode]
        block = block_at(mx, my, dx, dy)
        summed = p_ref[block, :, pl.ds(start, size)].astype(jnp.float32)
        for link in children(mode, dx, dy):
            slot = place_of(*moved(*link, dx, dy))
            pltpu.make_async_remote_copy(
                src_ref=stage[mode].at[slot],
                dst_ref=got[mode].at[slot],
                send_sem=send_sems.at[mode, slot],
                recv_sem=recv_sems.at[mode, slot],
                device_id={"tp": near[link]},
                device_id_type=pl.DeviceIdType.MESH,
            ).wait_recv()
            summed = summed + got[mode][slot].astype(jnp.float32)
        return summed

    def send(mode, dx, dy, source):
        slot = place_of(dx, dy)
        axis, sign = parent(mode, dx, dy)
        sent = pltpu.make_async_remote_copy(
            src_ref=source,
            dst_ref=got[mode].at[slot],
            send_sem=send_sems.at[mode, slot],
            recv_sem=recv_sems.at[mode, slot],
            device_id={"tp": near[axis, -sign]},
            device_id_type=pl.DeviceIdType.MESH,
        )
        sent.start()
        started.append(sent)

    def send_leaf(mode, dx, dy):
        start, size = parts[mode]
        send(mode, dx, dy, p_ref.at[block_at(mx, my, dx, dy), :, pl.ds(start, size)])

    def shift(mode):
        start, size = parts[mode]
        cols = pl.ds(start, size)
        return pltpu.make_async_remote_copy(
            src_ref=res_ref.at[:, cols],
            dst_ref=out_ref.at[:, cols],
            send_sem=shift_send.at[mode],
            recv_sem=shift_recv.at[mode],
            device_id={"section": after},
            device_id_type=pl.DeviceIdType.MESH,
        )

    order = arrival_order([part[1] * 16 / 46e3 for part in parts])[::-1]
    multiply(1)
    pl.semaphore_wait(barrier, len(near) + 1)
    early = [event for event in order[:16] if event[0] == 1 and not children(*event)]
    for event in early:
        send_leaf(*event)
    multiply(0)
    for event in order:
        if event in early:
            continue
        mode, dx, dy = event
        start, size = parts[mode]
        if (dx, dy) == (0, 0):
            cols = pl.ds(start, size)
            summed = total(mode, dx, dy) + hid_ref[:, cols].astype(jnp.float32)
            res_ref[:, cols] = summed.astype(jnp.bfloat16)
            shift(mode).start()
        elif children(mode, dx, dy):
            slot = place_of(dx, dy)
            stage[mode][slot] = total(mode, dx, dy).astype(jnp.bfloat16)
            send(mode, dx, dy, stage[mode].at[slot])
        else:
            send_leaf(mode, dx, dy)
    for sent in started:
        sent.wait_send()
    for mode in (0, 1):
        shift(mode).wait()


def reduce_rows(slot_tokens, heads, residual, weight_out):
    count, width = residual.shape
    groups = NX * NY
    parts = splits(width)
    vmem = pl.BlockSpec(memory_space=pltpu.VMEM)
    return pl.pallas_call(
        reduce_kernel,
        out_shape=jax.ShapeDtypeStruct((count, width), jnp.bfloat16),
        in_specs=[vmem, vmem, vmem, pl.BlockSpec(memory_space=pl.ANY)],
        out_specs=vmem,
        scratch_shapes=[
            pltpu.VMEM((groups, count, width), jnp.bfloat16),
            pltpu.VMEM(weight_out.shape, jnp.bfloat16),
            pltpu.VMEM((count, width), jnp.bfloat16),
            pltpu.VMEM((groups, count, parts[0][1]), jnp.bfloat16),
            pltpu.VMEM((groups, count, parts[1][1]), jnp.bfloat16),
            pltpu.VMEM((groups, count, parts[0][1]), jnp.bfloat16),
            pltpu.VMEM((groups, count, parts[1][1]), jnp.bfloat16),
            pltpu.SemaphoreType.DMA,
            pltpu.SemaphoreType.DMA((2,)),
            pltpu.SemaphoreType.DMA((2,)),
            pltpu.SemaphoreType.DMA((2, groups)),
            pltpu.SemaphoreType.DMA((2, groups)),
        ],
        compiler_params=pltpu.CompilerParams(collective_id=1, has_side_effects=True),
    )(slot_tokens, heads, residual, weight_out)


def owner_ranks(owners):
    count_all = owners.shape[0]
    same_owner = owners[:, None] == owners[None, :]
    position = jnp.arange(count_all, dtype=jnp.int32)
    earlier = position[None, :] < position[:, None]
    return jnp.sum(jnp.where(same_owner & earlier, 1, 0), axis=1).astype(jnp.int32)


def on_device(
    hidden, norm_gain, w_query, w_keyval, w_out, kv_cache, owner_map, accepted, context, draft_ids
):
    my_index = lax.axis_index("tp")
    owners = owner_map[0]
    accepts = accepted[0]
    lengths = context[0]
    token_ids = draft_ids[0]
    draft_steps = token_ids.shape[1]
    capacity = kv_cache.shape[1]
    slot_rows = capacity * draft_steps
    slot_of = owners * capacity + owner_ranks(owners)
    step_ids = jnp.arange(draft_steps, dtype=jnp.int32)
    slot_tokens = (slot_of[:, None] * draft_steps + step_ids[None, :]).reshape(1, -1)
    my_slots = my_index * capacity + jnp.arange(capacity, dtype=jnp.int32)
    mine = my_slots[:, None] == slot_of[None, :]
    my_lengths = jnp.sum(jnp.where(mine, lengths[None, :], 0), axis=1)
    my_accepts = jnp.sum(jnp.where(mine, accepts[None, :], 0), axis=1)
    my_ids = jnp.sum(jnp.where(mine[:, :, None], token_ids[None, :, :], 0), axis=1)
    outgoing = project_rows(
        hidden[0], norm_gain, slot_tokens, w_query[0], w_keyval[0], slot_rows
    )
    arrived = lax.all_to_all(outgoing, "tp", split_axis=0, concat_axis=0, tiled=True)
    attended, new_pairs = attend_slots(my_lengths, arrived, kv_cache[0])
    returned = lax.all_to_all(attended, "tp", split_axis=0, concat_axis=0, tiled=True)
    shifted = reduce_rows(slot_tokens, returned, hidden[0], w_out[0])
    keep = step_ids[None, :] < my_accepts[:, None]
    kept_ids = jnp.where(keep, my_ids, -1).reshape(-1)
    committed = jnp.where(keep.reshape(-1)[:, None], new_pairs, jnp.zeros_like(new_pairs))
    return (shifted[None], committed[None], kept_ids[None])


def solution(mesh):
    placed = (
        P("section", "tp", None),
        P("section", None),
        P("section", None, "tp"),
        P("section", "tp", None),
        P("section", "tp", None),
        P("section", "tp", None, None),
        P("section", None),
        P("section", None),
        P("section", None),
        P("section", None, None),
    )
    return jax.shard_map(
        on_device,
        mesh=mesh,
        in_specs=placed,
        out_specs=(P("section", "tp", None), P("section", "tp", None), P("section", "tp")),
        check_vma=False,
    )
```

time: 138 us -> 125 us (0.906)
  Pallas kernels: 68.5 us -> 89.6 us
  starting transfers between devices: 24.4 us -> 9.48 us
  matrix products: 10.2 us -> 0 us
  local copies, waits for them, and re-layouts: 9.77 us -> 4.31 us
  other arithmetic: 7.25 us -> 4.13 us
    pallas_call x1, Pallas kernels: 30.6 us -> 46.2 us  [reduce_rows(): pl.pallas_call(reduce_kernel, out_shape=jax.ShapeDtypeStruct((count, widt...]
    ppermute x1 -> x0, starting transfers between devices: 15 us -> none  [passed_along(): return lax.ppermute(block, axis, route)]
    dot_general x5 -> x0, matrix products: 10.2 us -> none  [the longest x1 4.52 us: on_device(): jnp.dot(row_piece, weight_query, preferred_element_type=jnp.float32)]
    pallas_call x1 -> x2, Pallas kernels: 37.9 us -> 43.4 us  [the longest x1 40.6 us: project_rows(): pl.pallas_call(project_kernel, out_shape=jax.ShapeDtypeStruct((groups, sl...]
    gather x6 -> x0, local copies, waits for them, and re-layouts: 5.42 us -> none  [the longest x1 1.95 us: on_device(): outgoing = jnp.take(projected, source, axis=0)]
    unnamed x18 -> x13, local copies, waits for them, and re-layouts: 0.8 us -> 2.94 us
    select_n x8 -> x1, other arithmetic: 1.86 us -> 0.07 us  [on_device(): kept_ids = jnp.where(keep, my_ids, -1).reshape(-1)]
    convert_element_type x1 -> x0, other arithmetic: 1.68 us -> none  [on_device(): (rows_f32 * inverse_rms * norm_gain[0][None, :]).astype(jnp.bfloat16)]
  transfers between devices with their start and end apart: 3 -> 2, of which waited for: 3 -> 2; matrix products, arithmetic and copies ran while one was open for 4% -> 3% of each run, Pallas kernels for 0% -> 0%
where the time goes in v2:
time: 125 us; the launch traced here: 124 us
  Pallas kernels  89.6 us (72%)
  waiting for transfers between devices  15.6 us (12%)
  starting transfers between devices  9.48 us (8%)
  local copies, waits for them, and re-layouts  4.31 us (3%)
  other arithmetic  4.13 us (3%)
    pallas_call x1, Pallas kernels, reduce_rows(): pl.pallas_call(reduce_kernel, out_shape=jax.ShapeDtypeStruct((count, widt...  46.2 us
    pallas_call x1, Pallas kernels, project_rows(): pl.pallas_call(project_kernel, out_shape=jax.ShapeDtypeStruct((groups, sl...  40.6 us
    all_to_all x1, waiting for transfers between devices, on_device(): lax.all_to_all(outgoing, 'tp', split_axis=0, concat_axis=0, tiled=True)  8.67 us
    all_to_all x1, waiting for transfers between devices, on_device(): lax.all_to_all(attended, 'tp', split_axis=0, concat_axis=0, tiled=True)  6.95 us
    all_to_all x1, starting transfers between devices, on_device(): lax.all_to_all(outgoing, 'tp', split_axis=0, concat_axis=0, tiled=True)  5.01 us
    all_to_all x1, starting transfers between devices, on_device(): lax.all_to_all(attended, 'tp', split_axis=0, concat_axis=0, tiled=True)  4.47 us
    unnamed x13, local copies, waits for them, and re-layouts  2.94 us
    pallas_call x1, Pallas kernels, attend_slots(): pl.pallas_call(attend_kernel, out_shape=(jax.ShapeDtypeStruct((groups, sl...  2.78 us
  transfers between devices with their start and end apart: 2, of which 2 were waited for; matrix products, arithmetic and copies ran while one was open for 3% of the time, Pallas kernels for 0%

profile of v2, /device:TPU:1, one launch (start us, length us, event | category | flops | bytes accessed | tf_op | source)
XLA Modules:
  0.0 123.9 jit_solution(8055069351596390975)
XLA Ops:
  0.6 0.0 copy-start.5
  0.6 0.0 copy-start.3
  0.7 0.0 copy-start.4
  0.7 0.0 copy-start.2
  0.7 0.9 select_reduce_fusion
  1.6 0.7 add_multiply_fusion
  2.3 0.1 iota_add_fusion
  2.4 0.7 add.47.slot_ref
  3.1 40.6 %shard_map.121 = bf16[32,16,256]{2,1,0:T(8,128)(2,1)} custom-call(bf16[8,8192]{1,0:T(8,128)(2,1)} %bitcast.21, f32[1,8192]{1,0:T(1,128)} %gain_ref.1, s32[1,256]{1,0:T(1,128)} %add.47.slot_ref, bf16[8192,128]{1,0:T(8,128)(2,1)} %bitcast.19, bf16[32,8192]{1,0:T(8,128)(2,1)} %bitcast.24), custom_call_target="tpu_custom_call" | custom-call | tf_op jit(solution)/shard_map/pallas_call | solution.py:225
  43.7 5.0 %all-to-all-start = ((bf16[32,16,256]{2,1,0:T(8,128)(2,1)}), bf16[32,16,256]{2,1,0:T(8,128)(2,1)S(1)}, u32[]{:S(2)}, u32[]{:S(2)}) async-start(bf16[32,16,256]{2,1,0:T(8,128)(2,1)} %shard_map.121), calls=%async_computation | async-start | bytes 524288 | tf_op jit(solution)/shard_map/all_to_all | solution.py:490
  48.7 0.0 copy-done.5
  48.7 0.0 copy-done.3
  48.7 0.0 copy-done.4
  48.8 0.7 select_reduce_fusion.2
  49.4 0.0 copy-done.2
  49.4 0.1 select_reduce_fusion.1
  49.6 0.1 broadcast_select_fusion
  49.7 8.7 %all-to-all-done.got_ref = bf16[32,16,256]{2,1,0:T(8,128)(2,1)S(1)} async-done(((bf16[32,16,256]{2,1,0:T(8,128)(2,1)}), bf16[32,16,256]{2,1,0:T(8,128)(2,1)S(1)}, u32[]{:S(2)}, u32[]{:S(2)}) %all-to-all-start) | async-done | bytes 262176 | tf_op jit(solution)/shard_map/all_to_all | solution.py:490
  58.3 0.0 copy-start
  58.3 0.7 copy-done
  59.0 2.8 %shard_map.122 = (bf16[32,16,128]{2,1,0:T(8,128)(2,1)}, bf16[16,1024]{1,0:T(8,128)(2,1)}) custom-call(s32[4]{0:T(128)} %get-tuple-element.8.len_ref, bf16[32,16,256]{2,1,0:T(8,128)(2,1)} %copy-done, bf16[96,1024]{1,0:T(8,128)(2,1)} %bitcast.25), custom_call_target="tpu_custom_call" | custom-call | tf_op jit(solution)/shard_map/pallas_call | solution.py:294
  61.8 4.5 %all-to-all-start.1 = ((bf16[32,16,128]{2,1,0:T(8,128)(2,1)}), bf16[32,16,128]{2,1,0:T(8,128)(2,1)S(1)}, u32[]{:S(2)}, u32[]{:S(2)}) async-start(bf16[32,16,128]{2,1,0:T(8,128)(2,1)} %get-tuple-element.5), calls=%async_computation.1 | async-start | bytes 262144 | tf_op jit(solution)/shard_map/all_to_all | solution.py:492
  66.3 0.1 iota_compare_fusion.1
  66.4 0.1 lt.47
  66.5 0.6 select_n.39
  67.1 1.4 %select_bitcast_fusion = bf16[1,16,1024]{2,1,0:T(8,128)(2,1)} fusion(bf16[16,1024]{1,0:T(8,128)(2,1)} %get-tuple-element.6, pred[16]{0:T(512)(128)(4,1)S(1)} %lt.47), kind=kLoop, calls=%fused_computation | loop fusion | flops 16384 | bytes 65552 | tf_op jit(solution)/shard_map/broadcast_in_dim | solution.py:497
  68.5 6.9 %all-to-all-done.1.heads_ref = bf16[32,16,128]{2,1,0:T(8,128)(2,1)S(1)} async-done(((bf16[32,16,128]{2,1,0:T(8,128)(2,1)}), bf16[32,16,128]{2,1,0:T(8,128)(2,1)S(1)}, u32[]{:S(2)}, u32[]{:S(2)}) %all-to-all-start.1) | async-done | bytes 131104 | tf_op jit(solution)/shard_map/all_to_all | solution.py:492
  75.4 0.0 copy-start.1
  75.4 0.7 copy-done.1
  76.1 46.2 %shard_map.123 = bf16[8,8192]{1,0:T(8,128)(2,1)} custom-call(s32[1,256]{1,0:T(1,128)} %add.47.slot_ref, bf16[32,16,128]{2,1,0:T(8,128)(2,1)} %copy-done.1, bf16[8,8192]{1,0:T(8,128)(2,1)} %bitcast.22, bf16[128,8192]{1,0:T(8,128)(2,1)} %bitcast.20), custom_call_target="tpu_custom_call" | custom-call | tf_op jit(solution)/shard_map/pallas_call | solution.py:437
  122.3 1.6 %copy.16 = bf16[1,8,8192]{2,1,0:T(8,128)(2,1)} copy(bf16[1,8,8192]{2,1,0:T(8,128)(2,1)} %bitcast.23) | data formatting | bytes 262144
  (2 shorter events, 0.0 us)
Async XLA Ops:
  0.6 48.1 %copy-start.5 = (s32[1,64]{1,0:T(1,128)S(1)}, s32[1,64]{1,0:T(1,128)}, u32[]{:S(2)}) copy-start(s32[1,64]{1,0:T(1,128)} %param.16) | copy-start | bytes 772
  0.6 48.1 %copy-start.3 = (s32[1,64]{1,0:T(1,128)S(1)}, s32[1,64]{1,0:T(1,128)}, u32[]{:S(2)}) copy-start(s32[1,64]{1,0:T(1,128)} %param.17) | copy-start | bytes 772
  0.7 48.1 %copy-start.4 = (s32[1,64]{1,0:T(1,128)S(1)}, s32[1,64]{1,0:T(1,128)}, u32[]{:S(2)}) copy-start(s32[1,64]{1,0:T(1,128)} %param.18) | copy-start | bytes 772
  0.7 48.8 %copy-start.2 = (s32[1,64,4]{1,2,0:T(4,128)S(1)}, s32[1,64,4]{1,2,0:T(4,128)}, u32[]{:S(2)}) copy-start(s32[1,64,4]{1,2,0:T(4,128)} %param.19) | copy-start | bytes 3076
  43.7 14.7 %all-to-all-start = ((bf16[32,16,256]{2,1,0:T(8,128)(2,1)}), bf16[32,16,256]{2,1,0:T(8,128)(2,1)S(1)}, u32[]{:S(2)}, u32[]{:S(2)}) async-start(bf16[32,16,256]{2,1,0:T(8,128)(2,1)} %shard_map.121), calls=%async_computation | async-start | bytes 524288 | tf_op jit(solution)/shard_map/all_to_all | solution.py:490
  58.3 0.7 copy-start
  61.8 13.6 %all-to-all-start.1 = ((bf16[32,16,128]{2,1,0:T(8,128)(2,1)}), bf16[32,16,128]{2,1,0:T(8,128)(2,1)S(1)}, u32[]{:S(2)}, u32[]{:S(2)}) async-start(bf16[32,16,128]{2,1,0:T(8,128)(2,1)} %get-tuple-element.5), calls=%async_computation.1 | async-start | bytes 262144 | tf_op jit(solution)/shard_map/all_to_all | solution.py:492
  75.4 0.7 copy-start.1

commit v3 on v2

--- a/solution.py
+++ b/solution.py
@@ -287,19 +287,82 @@
         ).astype(jnp.bfloat16)
 
 
-def attend_slots(lengths, arrived, cached):
-    groups, slot_rows, _ = arrived.shape
+def exchange_kernel(
+    len_ref, sent_ref, cache_ref, back_ref, pairs_ref,
+    got_ref, att_ref, send0, recv0, send1, recv1,
+):
+    me = lax.axis_index("tp")
+    groups = sent_ref.shape[0]
+    barrier = pltpu.get_barrier_semaphore()
+
+    def greet_one(i, carry):
+        pl.semaphore_signal(
+            barrier, inc=1, device_id={"tp": lax.rem(me + i, groups)},
+            device_id_type=pl.DeviceIdType.MESH,
+        )
+        return carry
+
+    lax.fori_loop(1, groups, greet_one, 0)
+    pl.semaphore_wait(barrier, groups - 1)
+
+    def exchange(source, target, send_sems, recv_sems):
+        def start(i, carry):
+            peer = lax.rem(me + i, groups)
+            pltpu.make_async_remote_copy(
+                src_ref=source.at[peer],
+                dst_ref=target.at[me],
+                send_sem=send_sems.at[i],
+                recv_sem=recv_sems.at[i],
+                device_id={"tp": peer},
+                device_id_type=pl.DeviceIdType.MESH,
+            ).start()
+            return carry
+
+        lax.fori_loop(1, groups, start, 0)
+        target[me] = source[me]
+
+        def finish(i, carry):
+            peer = lax.rem(me + i, groups)
+            origin = lax.rem(me + groups - i, groups)
+            pltpu.make_async_remote_copy(
+                src_ref=source.at[peer],
+                dst_ref=target.at[origin],
+                send_sem=send_sems.at[i],
+                recv_sem=recv_sems.at[i],
+                device_id={"tp": peer},
+                device_id_type=pl.DeviceIdType.MESH,
+            ).wait()
+            return carry
+
+        lax.fori_loop(1, groups, finish, 0)
+
+    exchange(sent_ref, got_ref, send0, recv0)
+    attend_kernel(len_ref, got_ref, cache_ref, att_ref, pairs_ref)
+    exchange(att_ref, back_ref, send1, recv1)
+
+
+def attend_slots(lengths, outgoing, cached):
+    groups, slot_rows, lanes = outgoing.shape
     slots, cached_len, width = cached.shape
     vmem = pl.BlockSpec(memory_space=pltpu.VMEM)
     return pl.pallas_call(
-        attend_kernel,
+        exchange_kernel,
         out_shape=(
             jax.ShapeDtypeStruct((groups, slot_rows, HD), jnp.bfloat16),
             jax.ShapeDtypeStruct((slot_rows, width), jnp.bfloat16),
         ),
         in_specs=[pl.BlockSpec(memory_space=pltpu.SMEM), vmem, vmem],
         out_specs=(vmem, vmem),
-    )(lengths, arrived, cached.reshape(slots * cached_len, width))
+        scratch_shapes=[
+            pltpu.VMEM((groups, slot_rows, lanes), jnp.bfloat16),
+            pltpu.VMEM((groups, slot_rows, HD), jnp.bfloat16),
+            pltpu.SemaphoreType.DMA((groups,)),
+            pltpu.SemaphoreType.DMA((groups,)),
+            pltpu.SemaphoreType.DMA((groups,)),
+            pltpu.SemaphoreType.DMA((groups,)),
+        ],
+        compiler_params=pltpu.CompilerParams(collective_id=2, has_side_effects=True),
+    )(lengths, outgoing, cached.reshape(slots * cached_len, width))
 
 
 def reduce_kernel(
@@ -487,9 +550,7 @@
     outgoing = project_rows(
         hidden[0], norm_gain, slot_tokens, w_query[0], w_keyval[0], slot_rows
     )
-    arrived = lax.all_to_all(outgoing, "tp", split_axis=0, concat_axis=0, tiled=True)
-    attended, new_pairs = attend_slots(my_lengths, arrived, kv_cache[0])
-    returned = lax.all_to_all(attended, "tp", split_axis=0, concat_axis=0, tiled=True)
+    returned, new_pairs = attend_slots(my_lengths, outgoing, kv_cache[0])
     shifted = reduce_rows(slot_tokens, returned, hidden[0], w_out[0])
     keep = step_ids[None, :] < my_accepts[:, None]
     kept_ids = jnp.where(keep, my_ids, -1).reshape(-1)

time: 125 us -> 119 us (0.952)
  Pallas kernels: 89.6 us -> 110 us
  waiting for transfers between devices: 15.6 us -> 0 us
  starting transfers between devices: 9.48 us -> 0 us
  local copies, waits for them, and re-layouts: 4.31 us -> 2.94 us
    pallas_call x1, Pallas kernels: 2.78 us -> 21.3 us  [attend_slots(): pl.pallas_call(exchange_kernel, out_shape=(jax.ShapeDtypeStruct((groups,...]
    all_to_all x2 -> x0, waiting for transfers between devices: 15.6 us -> none  [the longest x1 8.67 us: on_device(): lax.all_to_all(outgoing, 'tp', split_axis=0, concat_axis=0, tiled=True)]
    all_to_all x2 -> x0, starting transfers between devices: 9.48 us -> none  [the longest x1 5.01 us: on_device(): lax.all_to_all(outgoing, 'tp', split_axis=0, concat_axis=0, tiled=True)]
    pallas_call x1, Pallas kernels: 46.2 us -> 48.1 us  [reduce_rows(): pl.pallas_call(reduce_kernel, out_shape=jax.ShapeDtypeStruct((count, widt...]
    unnamed x13 -> x3, local copies, waits for them, and re-layouts: 2.94 us -> 1.57 us
  transfers between devices with their start and end apart: 2 -> 0, of which waited for: 2 -> 0; matrix products, arithmetic and copies ran while one was open for 3% -> 0% of each run, Pallas kernels for 0% -> 0%
where the time goes in v3:
time: 119 us
  Pallas kernels  110 us (92%)
  other arithmetic  5.34 us (4%)
  local copies, waits for them, and re-layouts  2.94 us (2%)
    pallas_call x1, Pallas kernels, reduce_rows(): pl.pallas_call(reduce_kernel, out_shape=jax.ShapeDtypeStruct((count, widt...  48.1 us
    pallas_call x1, Pallas kernels, project_rows(): pl.pallas_call(project_kernel, out_shape=jax.ShapeDtypeStruct((groups, sl...  40.6 us
    pallas_call x1, Pallas kernels, attend_slots(): pl.pallas_call(exchange_kernel, out_shape=(jax.ShapeDtypeStruct((groups,...  21.3 us

profile of v3, /device:TPU:1, one launch (start us, length us, event | category | flops | bytes accessed | tf_op | source)
XLA Modules:
  0.0 119.0 jit_solution(10350828118835601197)
XLA Ops:
  0.6 0.9 select_reduce_fusion
  1.6 0.7 fusion.1
  2.2 0.7 add_multiply_fusion
  2.9 1.4 %select_reduce_fusion.2 = (s32[4]{0:T(128)S(1)}, s32[4]{0:T(128)}, pred[4,64]{1,0:T(4,128)(4,1)S(1)}) fusion(s32[64]{0:T(128)} %bitcast.27, s32[64]{0:T(128)} %bitcast.28, s32[64]{0:T(128)S(1)} %fusion.1, s32[4]{0:T(128)S(1)} %iota_add_fusion.1), kind=kLoop, calls=%fused_computation.6 | loop fusion | flops 1272 | bytes 1072 | tf_op jit(solution)/shard_map/reduce_sum | solution.py:548
  4.2 0.1 iota_compare_fusion.1
  4.3 0.1 lt.47
  4.4 0.8 select_reduce_fusion.1
  5.2 0.1 broadcast_select_fusion
  5.3 0.6 select_n.39
  5.9 0.1 iota_add_fusion
  6.0 0.7 add.47.slot_ref
  6.7 40.6 %shard_map.121.sent_ref = bf16[32,16,256]{2,1,0:T(8,128)(2,1)} custom-call(bf16[8,8192]{1,0:T(8,128)(2,1)} %bitcast.21, f32[1,8192]{1,0:T(1,128)} %gain_ref.1, s32[1,256]{1,0:T(1,128)} %add.47.slot_ref, bf16[8192,128]{1,0:T(8,128)(2,1)} %bitcast.19, bf16[32,8192]{1,0:T(8,128)(2,1)} %bitcast.24), custom_call_target="tpu_custom_call" | custom-call | tf_op jit(solution)/shard_map/pallas_call | solution.py:225
  47.3 21.3 %shard_map.122 = (bf16[32,16,128]{2,1,0:T(8,128)(2,1)}, bf16[16,1024]{1,0:T(8,128)(2,1)}) custom-call(s32[4]{0:T(128)} %get-tuple-element.8.len_ref, bf16[32,16,256]{2,1,0:T(8,128)(2,1)} %shard_map.121.sent_ref, bf16[96,1024]{1,0:T(8,128)(2,1)} %bitcast.25), custom_call_target="tpu_custom_call" | custom-call | tf_op jit(solution)/shard_map/pallas_call | solution.py:348
  68.6 0.0 copy-start
  68.6 48.1 %shard_map.123 = bf16[8,8192]{1,0:T(8,128)(2,1)} custom-call(s32[1,256]{1,0:T(1,128)} %add.47.slot_ref, bf16[32,16,128]{2,1,0:T(8,128)(2,1)} %get-tuple-element.5.heads_ref, bf16[8,8192]{1,0:T(8,128)(2,1)} %bitcast.22, bf16[128,8192]{1,0:T(8,128)(2,1)} %bitcast.20), custom_call_target="tpu_custom_call" | custom-call | tf_op jit(solution)/shard_map/pallas_call | solution.py:500
  116.7 0.0 copy-done
  116.7 0.7 select_bitcast_fusion
  117.4 1.6 %copy.16 = bf16[1,8,8192]{2,1,0:T(8,128)(2,1)} copy(bf16[1,8,8192]{2,1,0:T(8,128)(2,1)} %bitcast.23) | data formatting | bytes 262144
  (1 shorter events, 0.0 us)
Async XLA Ops:
  68.6 48.1 %copy-start = (bf16[16,1024]{1,0:T(8,128)(2,1)S(1)}, bf16[16,1024]{1,0:T(8,128)(2,1)}, u32[]{:S(2)}) copy-start(bf16[16,1024]{1,0:T(8,128)(2,1)} %get-tuple-element.6) | copy-start | bytes 98308

commit v4 on v3

--- a/solution.py
+++ b/solution.py
@@ -112,14 +112,46 @@
     return lax.rem(mx + dx, NX) * NY + lax.rem(my + dy, NY)
 
 
-def slot_matrix(slot_ref, rows):
-    row = lax.broadcasted_iota(jnp.int32, (rows, slot_ref.shape[1]), 0)
-    return jnp.where(row == slot_ref[...], 1.0, 0.0).astype(jnp.bfloat16)
+def as_column(row):
+    size = row.shape[1]
+    first = lax.broadcasted_iota(jnp.int32, (size, size), 0)
+    second = lax.broadcasted_iota(jnp.int32, (size, size), 1)
+    return jnp.sum(jnp.where(first == second, row, 0), axis=1, keepdims=True)
+
+
+def slot_column(owners, capacity):
+    size = owners.shape[1]
+    column = as_column(owners)
+    request = lax.broadcasted_iota(jnp.int32, (size, size), 0)
+    other = lax.broadcasted_iota(jnp.int32, (size, size), 1)
+    earlier = (column == owners) & (other < request)
+    return column * capacity + jnp.sum(jnp.where(earlier, 1, 0), axis=1, keepdims=True)
+
+
+def as_row(column):
+    size = column.shape[0]
+    first = lax.broadcasted_iota(jnp.int32, (size, size), 0)
+    second = lax.broadcasted_iota(jnp.int32, (size, size), 1)
+    return jnp.sum(jnp.where(first == second, column, 0), axis=0, keepdims=True)
+
+
+def slot_matrix(owner_ref, tokens, rows):
+    owners = owner_ref[...]
+    requests = owners.shape[1]
+    steps = tokens // requests
+    capacity = rows // (NX * NY * steps)
+    column = slot_column(owners, capacity)
+    request = lax.broadcasted_iota(jnp.int32, (requests, tokens), 0)
+    token = lax.broadcasted_iota(jnp.int32, (requests, tokens), 1)
+    slots = jnp.sum(jnp.where(request == token // steps, column, 0), axis=0, keepdims=True)
+    step = lax.broadcasted_iota(jnp.int32, (1, tokens), 1) % steps
+    row = lax.broadcasted_iota(jnp.int32, (rows, tokens), 0)
+    return jnp.where(row == slots * steps + step, 1.0, 0.0).astype(jnp.bfloat16)
 
 
 def project_kernel(
-    hid_ref, gain_ref, slot_ref, wq_hbm, wp_hbm, out_ref,
-    x_ref, all_ref, wq_ref, wp_ref, acc_ref, load_sems, send_sems, recv_sems,
+    hid_ref, gain_ref, owner_ref, wq_hbm, wp_hbm, out_ref,
+    x_ref, all_ref, wq_ref, wp_ref, acc_ref, chosen_ref, load_sems, send_sems, recv_sems,
 ):
     me = lax.axis_index("tp")
     mx = me // NY
@@ -173,6 +205,7 @@
             started.append(sent)
         if len(started) == 8:
             all_ref[me] = x_ref[...]
+            chosen_ref[...] = slot_matrix(owner_ref, chosen_ref.shape[1], chosen_ref.shape[0])
             for load in loads:
                 load.wait()
     groups, count = all_ref.shape[:2]
@@ -201,7 +234,7 @@
     offset = lax.rem(me, LANES // pair_cols) * pair_cols
     spread = jnp.where(lane == source + offset, 1.0, 0.0).astype(jnp.bfloat16)
     placed = jnp.dot(pairs, spread, preferred_element_type=jnp.float32).astype(jnp.bfloat16)
-    chosen = slot_matrix(slot_ref, out_ref.shape[0] * out_ref.shape[1])
+    chosen = chosen_ref[...]
     out_shape = out_ref.shape[:2] + (LANES,)
     out_ref[:, :, :LANES] = (
         jnp.dot(chosen, queries, preferred_element_type=jnp.float32)
@@ -215,7 +248,7 @@
         sent.wait_send()
 
 
-def project_rows(hidden, gain, slot_tokens, weight_query, weight_pair, slot_rows):
+def project_rows(hidden, gain, owners, weight_query, weight_pair, slot_rows):
     count, width = hidden.shape
     groups = NX * NY
     vmem = pl.BlockSpec(memory_space=pltpu.VMEM)
@@ -233,30 +266,19 @@
             pltpu.VMEM(weight_query.shape, jnp.bfloat16),
             pltpu.VMEM(weight_pair.shape, jnp.bfloat16),
             pltpu.VMEM((groups * count, query_cols + pair_cols), jnp.float32),
+            pltpu.VMEM((groups * slot_rows, groups * count), jnp.bfloat16),
             pltpu.SemaphoreType.DMA((2,)),
             pltpu.SemaphoreType.DMA((2, groups)),
             pltpu.SemaphoreType.DMA((2, groups)),
         ],
         compiler_params=pltpu.CompilerParams(collective_id=0, has_side_effects=True),
-    )(hidden, gain, slot_tokens, weight_query, weight_pair)
-
-
-def attend_kernel(len_ref, got_ref, cache_ref, out_ref, pairs_ref):
+    )(hidden, gain, owners, weight_query, weight_pair)
+
+
+def attend_kernel(allowed, keep, got_ref, cache_ref, out_ref, pairs_ref):
     slot_rows = got_ref.shape[1]
-    slots = len_ref.shape[0]
-    steps = slot_rows // slots
-    cached_rows = cache_ref.shape[0]
-    cached_len = cached_rows // slots
-    span = cached_rows + slot_rows
     per_kv = HEADS // KVH
     rows = per_kv * slot_rows
-    row = lax.rem(lax.broadcasted_iota(jnp.int32, (rows, span), 0), slot_rows)
-    col = lax.broadcasted_iota(jnp.int32, (rows, span), 1)
-    fresh = col - cached_rows
-    allowed = (fresh >= 0) & (fresh // steps == row // steps) & (fresh <= row)
-    for slot in range(slots):
-        base = slot * cached_len
-        allowed |= (row // steps == slot) & (col >= base) & (col < base + len_ref[slot])
     pieces = got_ref.shape[0] // (2 * KVH)
     for e in range(KVH):
         cols = slice(e * HD, (e + 1) * HD)
@@ -270,8 +292,8 @@
 
         new_keys = joined(e * pieces)
         new_values = joined((KVH + e) * pieces)
-        pairs_ref[:, cols] = new_keys
-        pairs_ref[:, value_cols] = new_values
+        pairs_ref[:, cols] = jnp.where(keep, new_keys, jnp.zeros_like(new_keys))
+        pairs_ref[:, value_cols] = jnp.where(keep, new_values, jnp.zeros_like(new_values))
         keys = jnp.concatenate([cache_ref[:, cols], new_keys], axis=0)
         values = jnp.concatenate([cache_ref[:, value_cols], new_values], axis=0)
         queries = got_ref[e * per_kv : (e + 1) * per_kv, :, :LANES].reshape(rows, HD)
@@ -288,8 +310,8 @@
 
 
 def exchange_kernel(
-    len_ref, sent_ref, cache_ref, back_ref, pairs_ref,
-    got_ref, att_ref, send0, recv0, send1, recv1,
+    owner_ref, length_ref, accept_ref, id_ref, sent_ref, cache_ref,
+    back_ref, pairs_ref, kept_ref, got_ref, att_ref, send0, recv0, send1, recv1,
 ):
     me = lax.axis_index("tp")
     groups = sent_ref.shape[0]
@@ -303,6 +325,34 @@
         return carry
 
     lax.fori_loop(1, groups, greet_one, 0)
+    slot_rows = sent_ref.shape[1]
+    requests = owner_ref.shape[1]
+    steps = id_ref.shape[0]
+    slots = slot_rows // steps
+    cached_rows = cache_ref.shape[0]
+    cached_len = cached_rows // slots
+    slot_row = as_row(slot_column(owner_ref[...], slots))
+    row = lax.broadcasted_iota(jnp.int32, (slot_rows, requests), 0)
+    mine = me * slots + row // steps == slot_row
+    ids = jnp.zeros((slot_rows, requests), jnp.int32)
+    for j in range(steps):
+        ids = jnp.where(row % steps == j, id_ref[j : j + 1, :], ids)
+
+    def held(values):
+        return jnp.sum(jnp.where(mine, values, 0), axis=1, keepdims=True)
+
+    lengths = held(length_ref[...])
+    step = lax.broadcasted_iota(jnp.int32, (slot_rows, 1), 0) % steps
+    keep = step < held(accept_ref[...])
+    kept_ref[...] = as_row(jnp.where(keep, held(ids), -1))
+    span = cached_rows + slot_rows
+    row = lax.broadcasted_iota(jnp.int32, (slot_rows, span), 0)
+    col = lax.broadcasted_iota(jnp.int32, (slot_rows, span), 1)
+    fresh = col - cached_rows
+    in_cache = (fresh < 0) & (col // cached_len == row // steps) & (col % cached_len < lengths)
+    in_draft = (fresh >= 0) & (fresh // steps == row // steps) & (fresh <= row)
+    flags = jnp.where(in_cache | in_draft, 1, 0)
+    allowed = jnp.concatenate([flags] * (HEADS // KVH), axis=0) == 1
     pl.semaphore_wait(barrier, groups - 1)
 
     def exchange(source, target, send_sems, recv_sems):
@@ -337,11 +387,11 @@
         lax.fori_loop(1, groups, finish, 0)
 
     exchange(sent_ref, got_ref, send0, recv0)
-    attend_kernel(len_ref, got_ref, cache_ref, att_ref, pairs_ref)
+    attend_kernel(allowed, keep, got_ref, cache_ref, att_ref, pairs_ref)
     exchange(att_ref, back_ref, send1, recv1)
 
 
-def attend_slots(lengths, outgoing, cached):
+def attend_slots(owners, lengths, accepts, ids, outgoing, cached):
     groups, slot_rows, lanes = outgoing.shape
     slots, cached_len, width = cached.shape
     vmem = pl.BlockSpec(memory_space=pltpu.VMEM)
@@ -350,9 +400,10 @@
         out_shape=(
             jax.ShapeDtypeStruct((groups, slot_rows, HD), jnp.bfloat16),
             jax.ShapeDtypeStruct((slot_rows, width), jnp.bfloat16),
+            jax.ShapeDtypeStruct((1, slot_rows), jnp.int32),
         ),
-        in_specs=[pl.BlockSpec(memory_space=pltpu.SMEM), vmem, vmem],
-        out_specs=(vmem, vmem),
+        in_specs=[vmem] * 6,
+        out_specs=(vmem, vmem, vmem),
         scratch_shapes=[
             pltpu.VMEM((groups, slot_rows, lanes), jnp.bfloat16),
             pltpu.VMEM((groups, slot_rows, HD), jnp.bfloat16),
@@ -362,11 +413,11 @@
             pltpu.SemaphoreType.DMA((groups,)),
         ],
         compiler_params=pltpu.CompilerParams(collective_id=2, has_side_effects=True),
-    )(lengths, outgoing, cached.reshape(slots * cached_len, width))
+    )(owners, lengths, accepts, ids, outgoing, cached.reshape(slots * cached_len, width))
 
 
 def reduce_kernel(
-    slot_ref, heads_ref, hid_ref, wo_hbm, out_ref,
+    owner_ref, heads_ref, hid_ref, wo_hbm, out_ref,
     p_ref, wo_ref, res_ref, got0, got1, stage0, stage1,
     load_sem, shift_send, shift_recv, send_sems, recv_sems,
 ):
@@ -395,7 +446,7 @@
     groups, count = p_ref.shape[:2]
     tokens = groups * count
     slot_rows = heads_ref.shape[0] * heads_ref.shape[1]
-    chosen = slot_matrix(slot_ref, slot_rows)
+    chosen = slot_matrix(owner_ref, tokens, slot_rows)
     heads = lax.dot_general(
         chosen, heads_ref[...].reshape(slot_rows, heads_ref.shape[2]),
         (((0,), (0,)), ((), ())), preferred_element_type=jnp.float32,
@@ -492,7 +543,7 @@
         shift(mode).wait()
 
 
-def reduce_rows(slot_tokens, heads, residual, weight_out):
+def reduce_rows(owners, heads, residual, weight_out):
     count, width = residual.shape
     groups = NX * NY
     parts = splits(width)
@@ -517,45 +568,21 @@
             pltpu.SemaphoreType.DMA((2, groups)),
         ],
         compiler_params=pltpu.CompilerParams(collective_id=1, has_side_effects=True),
-    )(slot_tokens, heads, residual, weight_out)
-
-
-def owner_ranks(owners):
-    count_all = owners.shape[0]
-    same_owner = owners[:, None] == owners[None, :]
-    position = jnp.arange(count_all, dtype=jnp.int32)
-    earlier = position[None, :] < position[:, None]
-    return jnp.sum(jnp.where(same_owner & earlier, 1, 0), axis=1).astype(jnp.int32)
+    )(owners, heads, residual, weight_out)
 
 
 def on_device(
     hidden, norm_gain, w_query, w_keyval, w_out, kv_cache, owner_map, accepted, context, draft_ids
 ):
-    my_index = lax.axis_index("tp")
-    owners = owner_map[0]
-    accepts = accepted[0]
-    lengths = context[0]
-    token_ids = draft_ids[0]
-    draft_steps = token_ids.shape[1]
-    capacity = kv_cache.shape[1]
-    slot_rows = capacity * draft_steps
-    slot_of = owners * capacity + owner_ranks(owners)
-    step_ids = jnp.arange(draft_steps, dtype=jnp.int32)
-    slot_tokens = (slot_of[:, None] * draft_steps + step_ids[None, :]).reshape(1, -1)
-    my_slots = my_index * capacity + jnp.arange(capacity, dtype=jnp.int32)
-    mine = my_slots[:, None] == slot_of[None, :]
-    my_lengths = jnp.sum(jnp.where(mine, lengths[None, :], 0), axis=1)
-    my_accepts = jnp.sum(jnp.where(mine, accepts[None, :], 0), axis=1)
-    my_ids = jnp.sum(jnp.where(mine[:, :, None], token_ids[None, :, :], 0), axis=1)
+    slot_rows = kv_cache.shape[1] * draft_ids.shape[2]
     outgoing = project_rows(
-        hidden[0], norm_gain, slot_tokens, w_query[0], w_keyval[0], slot_rows
+        hidden[0], norm_gain, owner_map, w_query[0], w_keyval[0], slot_rows
     )
-    returned, new_pairs = attend_slots(my_lengths, outgoing, kv_cache[0])
-    shifted = reduce_rows(slot_tokens, returned, hidden[0], w_out[0])
-    keep = step_ids[None, :] < my_accepts[:, None]
-    kept_ids = jnp.where(keep, my_ids, -1).reshape(-1)
-    committed = jnp.where(keep.reshape(-1)[:, None], new_pairs, jnp.zeros_like(new_pairs))
-    return (shifted[None], committed[None], kept_ids[None])
+    returned, committed, kept_ids = attend_slots(
+        owner_map, context, accepted, draft_ids[0].T, outgoing, kv_cache[0]
+    )
+    shifted = reduce_rows(owner_map, returned, hidden[0], w_out[0])
+    return (shifted[None], committed[None], kept_ids)
 
 
 def solution(mesh):

time: 119 us -> 113 us (0.950)
  other arithmetic: 5.34 us -> 0 us
    reduce_sum x3 -> x0, other arithmetic: 3.1 us -> none  [the longest x1 1.37 us: on_device(): my_accepts = jnp.sum(jnp.where(mine, accepts[None, :], 0), axis=1)]
    unnamed x3 -> x7, local copies, waits for them, and re-layouts: 1.57 us -> 2.7 us
where the time goes in v4:
time: 113 us
  Pallas kernels  109 us (96%)
  local copies, waits for them, and re-layouts  2.7 us (2%)
    pallas_call x1, Pallas kernels, reduce_rows(): pl.pallas_call(reduce_kernel, out_shape=jax.ShapeDtypeStruct((count, widt...  47.8 us
    pallas_call x1, Pallas kernels, project_rows(): pl.pallas_call(project_kernel, out_shape=jax.ShapeDtypeStruct((groups, sl...  40.6 us
    pallas_call x1, Pallas kernels, attend_slots(): pl.pallas_call(exchange_kernel, out_shape=(jax.ShapeDtypeStruct((groups,...  21.1 us
    unnamed x7, local copies, waits for them, and re-layouts  2.7 us

profile of v4, /device:TPU:1, one launch (start us, length us, event | category | flops | bytes accessed | tf_op | source)
XLA Modules:
  0.0 112.8 jit_solution(4824136516813694999)
XLA Ops:
  0.6 40.6 %shard_map.121.sent_ref = bf16[32,16,256]{2,1,0:T(8,128)(2,1)} custom-call(bf16[8,8192]{1,0:T(8,128)(2,1)} %bitcast.13, f32[1,8192]{1,0:T(1,128)} %gain_ref.1, s32[1,64]{1,0:T(1,128)} %owner_ref.5, bf16[8192,128]{1,0:T(8,128)(2,1)} %bitcast.10, bf16[32,8192]{1,0:T(8,128)(2,1)} %bitcast.12), custom_call_target="tpu_custom_call" | custom-call | tf_op jit(solution)/shard_map/pallas_call | solution.py:258
  41.2 21.1 %shard_map.122 = (bf16[32,16,128]{2,1,0:T(8,128)(2,1)}, bf16[16,1024]{1,0:T(8,128)(2,1)}, s32[1,16]{1,0:T(1,128)}) custom-call(s32[1,64]{1,0:T(1,128)} %owner_ref.5, s32[1,64]{1,0:T(1,128)} %length_ref.1, s32[1,64]{1,0:T(1,128)} %accept_ref.1, s32[4,64]{1,0:T(4,128)} %bitcast.18, bf16[32,16,256]{2,1,0:T(8,128)(2,1)} %shard_map.121.sent_ref, ...), custom_call_target="tpu_custom_call" | custom-call | tf_op jit(solution)/shard_map/pallas_call | solution.py:398
  62.3 0.0 copy-start
  62.3 0.0 copy-start.1
  62.4 47.8 %shard_map.123 = bf16[8,8192]{1,0:T(8,128)(2,1)} custom-call(s32[1,64]{1,0:T(1,128)} %owner_ref.5, bf16[32,16,128]{2,1,0:T(8,128)(2,1)} %get-tuple-element.6.heads_ref, bf16[8,8192]{1,0:T(8,128)(2,1)} %bitcast.14, bf16[128,8192]{1,0:T(8,128)(2,1)} %bitcast.11), custom_call_target="tpu_custom_call" | custom-call | tf_op jit(solution)/shard_map/pallas_call | solution.py:551
  110.1 1.6 %copy.16 = bf16[1,8,8192]{2,1,0:T(8,128)(2,1)} copy(bf16[1,8,8192]{2,1,0:T(8,128)(2,1)} %bitcast.15) | data formatting | bytes 262144
  111.7 0.0 copy-done
  111.7 0.6 copy.17
  112.3 0.0 copy-done.1
  112.3 0.5 copy.18
Async XLA Ops:
  62.3 49.4 %copy-start = (bf16[16,1024]{1,0:T(8,128)(2,1)S(1)}, bf16[16,1024]{1,0:T(8,128)(2,1)}, u32[]{:S(2)}) copy-start(bf16[16,1024]{1,0:T(8,128)(2,1)} %get-tuple-element.7) | copy-start | bytes 98308
  62.3 50.0 %copy-start.1 = (s32[1,16]{1,0:T(1,128)S(1)}, s32[1,16]{1,0:T(1,128)}, u32[]{:S(2)}) copy-start(s32[1,16]{1,0:T(1,128)} %get-tuple-element.14) | copy-start | bytes 196

commit v5 on v4

--- a/solution.py
+++ b/solution.py
@@ -151,7 +151,7 @@
 
 def project_kernel(
     hid_ref, gain_ref, owner_ref, wq_hbm, wp_hbm, out_ref,
-    x_ref, all_ref, wq_ref, wp_ref, acc_ref, chosen_ref, load_sems, send_sems, recv_sems,
+    x_ref, all_ref, wq_ref, wp_ref, turned_ref, acc_ref, chosen_ref, load_sems, send_sems, recv_sems,
 ):
     me = lax.axis_index("tp")
     mx = me // NY
@@ -208,6 +208,10 @@
             chosen_ref[...] = slot_matrix(owner_ref, chosen_ref.shape[1], chosen_ref.shape[0])
             for load in loads:
                 load.wait()
+            turned_ref[...] = jnp.zeros_like(turned_ref)
+            for k in range(8):
+                cols = pl.ds(k * (width // 8), width // 8)
+                turned_ref[cols, : wp_ref.shape[0]] = wp_ref[:, cols].T
     groups, count = all_ref.shape[:2]
     tokens = groups * count
     query_cols = wq_ref.shape[1]
@@ -218,17 +222,13 @@
     def add(k, carry):
         cols = pl.ds(pl.multiple_of(k * step, step), step)
         x = all_ref[:, :, cols].reshape(tokens, step)
-        acc_ref[:, :query_cols] += jnp.dot(
-            x, wq_ref[cols, :], preferred_element_type=jnp.float32
-        )
-        acc_ref[:, query_cols:] += lax.dot_general(
-            x, wp_ref[:, cols], (((1,), (1,)), ((), ())), preferred_element_type=jnp.float32
-        )
+        weights = jnp.concatenate([wq_ref[cols, :], turned_ref[cols, :]], axis=1)
+        acc_ref[...] += jnp.dot(x, weights, preferred_element_type=jnp.float32)
         return carry
 
     lax.fori_loop(0, 8, add, 0)
     queries = acc_ref[:, :query_cols].astype(jnp.bfloat16)
-    pairs = acc_ref[:, query_cols:].astype(jnp.bfloat16)
+    pairs = acc_ref[:, query_cols : query_cols + pair_cols].astype(jnp.bfloat16)
     lane = lax.broadcasted_iota(jnp.int32, (pair_cols, LANES), 1)
     source = lax.broadcasted_iota(jnp.int32, (pair_cols, LANES), 0)
     offset = lax.rem(me, LANES // pair_cols) * pair_cols
@@ -254,7 +254,6 @@
     vmem = pl.BlockSpec(memory_space=pltpu.VMEM)
     hbm = pl.BlockSpec(memory_space=pl.ANY)
     query_cols = weight_query.shape[1]
-    pair_cols = weight_pair.shape[0]
     return pl.pallas_call(
         project_kernel,
         out_shape=jax.ShapeDtypeStruct((groups, slot_rows, 2 * LANES), jnp.bfloat16),
@@ -265,7 +264,8 @@
             pltpu.VMEM((groups, count, width), jnp.bfloat16),
             pltpu.VMEM(weight_query.shape, jnp.bfloat16),
             pltpu.VMEM(weight_pair.shape, jnp.bfloat16),
-            pltpu.VMEM((groups * count, query_cols + pair_cols), jnp.float32),
+            pltpu.VMEM((width, LANES), jnp.bfloat16),
+            pltpu.VMEM((groups * count, query_cols + LANES), jnp.float32),
             pltpu.VMEM((groups * slot_rows, groups * count), jnp.bfloat16),
             pltpu.SemaphoreType.DMA((2,)),
             pltpu.SemaphoreType.DMA((2, groups)),
@@ -463,7 +463,7 @@
             p_ref[:, :, cols] = piece.reshape(groups, count, step).astype(jnp.bfloat16)
             return carry
 
-        lax.fori_loop(0, size // step, one, 0)
+        lax.fori_loop(0, size // step, one, 0, unroll=True)
 
     started = []
 

time: 113 us -> 113 us (level)
  no operation moved by 1% of the time
where the time goes in v5:
time: 113 us; the launch traced here: 112 us
  Pallas kernels  109 us (96%)
  local copies, waits for them, and re-layouts  2.7 us (2%)
    pallas_call x1, Pallas kernels, reduce_rows(): pl.pallas_call(reduce_kernel, out_shape=jax.ShapeDtypeStruct((count, widt...  47.9 us
    pallas_call x1, Pallas kernels, project_rows(): pl.pallas_call(project_kernel, out_shape=jax.ShapeDtypeStruct((groups, sl...  39.7 us
    pallas_call x1, Pallas kernels, attend_slots(): pl.pallas_call(exchange_kernel, out_shape=(jax.ShapeDtypeStruct((groups,...  21.1 us
    unnamed x7, local copies, waits for them, and re-layouts  2.7 us

profile of v5, /device:TPU:1, one launch (start us, length us, event | category | flops | bytes accessed | tf_op | source)
XLA Modules:
  0.0 112.0 jit_solution(14571604610164093015)
XLA Ops:
  0.6 39.7 %shard_map.121.sent_ref = bf16[32,16,256]{2,1,0:T(8,128)(2,1)} custom-call(bf16[8,8192]{1,0:T(8,128)(2,1)} %bitcast.13, f32[1,8192]{1,0:T(1,128)} %gain_ref.1, s32[1,64]{1,0:T(1,128)} %owner_ref.5, bf16[8192,128]{1,0:T(8,128)(2,1)} %bitcast.10, bf16[32,8192]{1,0:T(8,128)(2,1)} %bitcast.12), custom_call_target="tpu_custom_call" | custom-call | tf_op jit(solution)/shard_map/pallas_call | solution.py:257
  40.3 21.1 %shard_map.122 = (bf16[32,16,128]{2,1,0:T(8,128)(2,1)}, bf16[16,1024]{1,0:T(8,128)(2,1)}, s32[1,16]{1,0:T(1,128)}) custom-call(s32[1,64]{1,0:T(1,128)} %owner_ref.5, s32[1,64]{1,0:T(1,128)} %length_ref.1, s32[1,64]{1,0:T(1,128)} %accept_ref.1, s32[4,64]{1,0:T(4,128)} %bitcast.18, bf16[32,16,256]{2,1,0:T(8,128)(2,1)} %shard_map.121.sent_ref, ...), custom_call_target="tpu_custom_call" | custom-call | tf_op jit(solution)/shard_map/pallas_call | solution.py:398
  61.4 0.0 copy-start
  61.4 0.0 copy-start.1
  61.4 47.9 %shard_map.123 = bf16[8,8192]{1,0:T(8,128)(2,1)} custom-call(s32[1,64]{1,0:T(1,128)} %owner_ref.5, bf16[32,16,128]{2,1,0:T(8,128)(2,1)} %get-tuple-element.6.heads_ref, bf16[8,8192]{1,0:T(8,128)(2,1)} %bitcast.14, bf16[128,8192]{1,0:T(8,128)(2,1)} %bitcast.11), custom_call_target="tpu_custom_call" | custom-call | tf_op jit(solution)/shard_map/pallas_call | solution.py:551
  109.3 1.6 %copy.16 = bf16[1,8,8192]{2,1,0:T(8,128)(2,1)} copy(bf16[1,8,8192]{2,1,0:T(8,128)(2,1)} %bitcast.15) | data formatting | bytes 262144
  110.9 0.0 copy-done
  110.9 0.6 copy.17
  111.5 0.0 copy-done.1
  111.5 0.5 copy.18
Async XLA Ops:
  61.4 49.5 %copy-start = (bf16[16,1024]{1,0:T(8,128)(2,1)S(1)}, bf16[16,1024]{1,0:T(8,128)(2,1)}, u32[]{:S(2)}) copy-start(bf16[16,1024]{1,0:T(8,128)(2,1)} %get-tuple-element.7) | copy-start | bytes 98308
  61.4 50.1 %copy-start.1 = (s32[1,16]{1,0:T(1,128)S(1)}, s32[1,16]{1,0:T(1,128)}, u32[]{:S(2)}) copy-start(s32[1,16]{1,0:T(1,128)} %get-tuple-element.14) | copy-start | bytes 196

commit v6 on v5

--- a/solution.py
+++ b/solution.py
@@ -226,7 +226,7 @@
         acc_ref[...] += jnp.dot(x, weights, preferred_element_type=jnp.float32)
         return carry
 
-    lax.fori_loop(0, 8, add, 0)
+    lax.fori_loop(0, 8, add, 0, unroll=True)
     queries = acc_ref[:, :query_cols].astype(jnp.bfloat16)
     pairs = acc_ref[:, query_cols : query_cols + pair_cols].astype(jnp.bfloat16)
     lane = lax.broadcasted_iota(jnp.int32, (pair_cols, LANES), 1)

time: 113 us -> 112 us (level)
  Pallas kernels: 109 us -> 107 us
where the time goes in v6:
time: 112 us; the launch traced here: 111 us
  Pallas kernels  107 us (96%)
  local copies, waits for them, and re-layouts  2.7 us (2%)
    pallas_call x1, Pallas kernels, reduce_rows(): pl.pallas_call(reduce_kernel, out_shape=jax.ShapeDtypeStruct((count, widt...  47.7 us
    pallas_call x1, Pallas kernels, project_rows(): pl.pallas_call(project_kernel, out_shape=jax.ShapeDtypeStruct((groups, sl...  38.6 us
    pallas_call x1, Pallas kernels, attend_slots(): pl.pallas_call(exchange_kernel, out_shape=(jax.ShapeDtypeStruct((groups,...  21.1 us
    unnamed x7, local copies, waits for them, and re-layouts  2.7 us

profile of v6, /device:TPU:1, one launch (start us, length us, event | category | flops | bytes accessed | tf_op | source)
XLA Modules:
  0.0 110.8 jit_solution(15236206163068763783)
XLA Ops:
  0.6 38.6 %shard_map.121.sent_ref = bf16[32,16,256]{2,1,0:T(8,128)(2,1)} custom-call(bf16[8,8192]{1,0:T(8,128)(2,1)} %bitcast.13, f32[1,8192]{1,0:T(1,128)} %gain_ref.1, s32[1,64]{1,0:T(1,128)} %owner_ref.5, bf16[8192,128]{1,0:T(8,128)(2,1)} %bitcast.10, bf16[32,8192]{1,0:T(8,128)(2,1)} %bitcast.12), custom_call_target="tpu_custom_call" | custom-call | tf_op jit(solution)/shard_map/pallas_call | solution.py:257
  39.2 21.1 %shard_map.122 = (bf16[32,16,128]{2,1,0:T(8,128)(2,1)}, bf16[16,1024]{1,0:T(8,128)(2,1)}, s32[1,16]{1,0:T(1,128)}) custom-call(s32[1,64]{1,0:T(1,128)} %owner_ref.5, s32[1,64]{1,0:T(1,128)} %length_ref.1, s32[1,64]{1,0:T(1,128)} %accept_ref.1, s32[4,64]{1,0:T(4,128)} %bitcast.18, bf16[32,16,256]{2,1,0:T(8,128)(2,1)} %shard_map.121.sent_ref, ...), custom_call_target="tpu_custom_call" | custom-call | tf_op jit(solution)/shard_map/pallas_call | solution.py:398
  60.3 0.0 copy-start
  60.3 0.0 copy-start.1
  60.3 47.7 %shard_map.123 = bf16[8,8192]{1,0:T(8,128)(2,1)} custom-call(s32[1,64]{1,0:T(1,128)} %owner_ref.5, bf16[32,16,128]{2,1,0:T(8,128)(2,1)} %get-tuple-element.6.heads_ref, bf16[8,8192]{1,0:T(8,128)(2,1)} %bitcast.14, bf16[128,8192]{1,0:T(8,128)(2,1)} %bitcast.11), custom_call_target="tpu_custom_call" | custom-call | tf_op jit(solution)/shard_map/pallas_call | solution.py:551
  108.1 1.6 %copy.16 = bf16[1,8,8192]{2,1,0:T(8,128)(2,1)} copy(bf16[1,8,8192]{2,1,0:T(8,128)(2,1)} %bitcast.15) | data formatting | bytes 262144
  109.6 0.0 copy-done
  109.6 0.6 copy.17
  110.3 0.0 copy-done.1
  110.3 0.5 copy.18
Async XLA Ops:
  60.3 49.3 %copy-start = (bf16[16,1024]{1,0:T(8,128)(2,1)S(1)}, bf16[16,1024]{1,0:T(8,128)(2,1)}, u32[]{:S(2)}) copy-start(bf16[16,1024]{1,0:T(8,128)(2,1)} %get-tuple-element.7) | copy-start | bytes 98308
  60.3 49.9 %copy-start.1 = (s32[1,16]{1,0:T(1,128)S(1)}, s32[1,16]{1,0:T(1,128)}, u32[]{:S(2)}) copy-start(s32[1,16]{1,0:T(1,128)} %get-tuple-element.14) | copy-start | bytes 196
